TPU v7x, 32 devices: a whole 2x2x4 slice. The times are simulated.
32 devices in a mesh: gx: 4 (over y, x), gy: 8 (over z, core).
Axes of the slice: x: 2, y: 2, z: 4, core: 2. Of those that a mesh axis runs over, the one named last changes fastest.
Arguments:
- right_side: float32 [8, 3, 64, 1024], P(None, None, 'gx', 'gy'), may hold values from -50 to 50
- first_guess: float32 [8, 3, 64, 1024], P(None, None, 'gx', 'gy'), may hold values from -3 to 3
- diag_block: bfloat16 [8, 3, 3, 64, 1024], P(None, None, None, 'gx', 'gy'), may hold values from -2.41 to 12
- mobility: bfloat16 [8, 3, 3, 64, 1024], P(None, None, None, 'gx', 'gy'), may hold values from -1 to 1.21
- face_trans: bfloat16 [6, 8, 64, 1024], P(None, None, 'gx', 'gy'), may hold values from 0.19921875 to 1
- column_inverse: bfloat16 [4, 6, 6, 64, 1024], P(None, None, None, 'gx', 'gy'), may hold values from -0.061 to 0.201
- perf_cell: int32 [32, 32, 40], P(('gx', 'gy')), may hold values from 0 to 16383, as said below
- perf_slot: int32 [32, 32, 40], P(('gx', 'gy')), may hold values from 0 to 1024, as said below
- well_in: float32 [3, 32768], P(None, ('gx', 'gy')), may hold values from -4 to 4
- well_out: float32 [3, 32768], P(None, ('gx', 'gy')), may hold values from -4 to 4
- well_inverse: float32 [256, 128, 128], P(('gx', 'gy')), may hold values from -1 to 1
Outputs:
- solution: float32 [8, 3, 64, 1024], P(None, None, 'gx', 'gy')
- residual: float32 [8, 3, 64, 1024], P(None, None, 'gx', 'gy')
Inputs may be any that keep to these rules, and one draw needn't show every extreme that they name: `perf_cell`: entry [s, d, q] is a local cell number of device s's tile, the cell of slot q from device s to owner d; the slot's segment is perf_slot[d, s, q]; slots that perf_slot marks empty carry an arbitrary cell. `perf_slot`: entry [d, s, q] is w * 128 + g when slot q from device s carries segment g of owner d's local well w, and 1024 when the slot is empty. Each segment of an owner appears at most once; the segments of a well that appear are 0 to n - 1 for its padded count n of 1 to 128. Every pair (d, s) has at most 40 live slots and some pair has exactly 40; in every draw some owner has all 1024 segments live.
All inputs are finite; a program needn't handle non-finite values.
Results may differ from a plain program's by a relative error of at most 0.0003.
Values sent between devices are 32-bit elements; how exact they have to be, the bound alone decides.
No kernel may reach another device: no remote copies, remote signals or barrier semaphores. Data moves between devices by JAX's collectives and lax.ppermute only.
A program may use at most 128 MiB of HBM per device.

v0:
```python
import jax
import jax.numpy as jnp
from jax import lax
from jax.sharding import PartitionSpec as P

ITERS = 2


def padded_2(block, sides, width):
    for axis, dim in sides:
        count = lax.axis_size(axis)
        forward = [(i, i + 1) for i in range(count - 1)]
        backward = [(target, source) for source, target in forward]
        low = lax.ppermute(
            lax.slice_in_dim(block, block.shape[dim] - width, None, axis=dim), axis, forward
        )
        high = lax.ppermute(lax.slice_in_dim(block, 0, width, axis=dim), axis, backward)
        block = jnp.concatenate([low, block, high], axis=dim)
    return block


def couple(mixing, vector):
    summed = mixing[:, :, 0].astype(jnp.float32) * vector[:, 0:1]
    summed = summed + mixing[:, :, 1].astype(jnp.float32) * vector[:, 1:2]
    summed = summed + mixing[:, :, 2].astype(jnp.float32) * vector[:, 2:3]
    return summed


def stencil(vector, extended, diag_block, face_trans):
    factor = face_trans.astype(jnp.float32)[:, :, None]
    interior = extended[:, :, 1:-1, 1:-1]
    zero_layer = jnp.zeros_like(interior[:1])
    under_layer = jnp.concatenate([zero_layer, interior[:-1]], axis=0)
    over_layer = jnp.concatenate([interior[1:], zero_layer], axis=0)
    beside = factor[0] * extended[:, :, :-2, 1:-1]
    beside = beside + factor[1] * extended[:, :, 2:, 1:-1]
    beside = beside + factor[2] * extended[:, :, 1:-1, :-2]
    beside = beside + factor[3] * extended[:, :, 1:-1, 2:]
    beside = beside + factor[4] * under_layer
    beside = beside + factor[5] * over_layer
    return couple(diag_block, vector) - beside


def precondition(vector, column_inverse):
    layers, comps, tile_rows, tile_cols = vector.shape
    paired = vector.reshape(layers // 2, 6, tile_rows, tile_cols)
    result = column_inverse[:, :, 0].astype(jnp.float32) * paired[:, 0:1]
    for member in range(1, 6):
        result = (
            result
            + column_inverse[:, :, member].astype(jnp.float32) * paired[:, member : member + 1]
        )
    return result.reshape(vector.shape)


def per_device(
    right_side,
    first_guess,
    diag_block,
    mobility,
    face_trans,
    column_inverse,
    perf_cell,
    perf_slot,
    well_in,
    well_out,
    well_inverse,
):
    layers, comps, tile_rows, tile_cols = right_side.shape
    tile_area = tile_rows * tile_cols
    cell_ids = perf_cell[0]
    targets = perf_slot[0]
    layer_idx = cell_ids // tile_area
    column_idx = cell_ids % tile_area
    well_count = well_inverse.shape[0]
    seg_count = well_inverse.shape[1]
    per_owner = well_count * seg_count
    pad_in = jnp.concatenate([well_in, jnp.zeros((3, 1), jnp.float32)], axis=1)
    pad_out = jnp.concatenate([well_out, jnp.zeros((3, 1), jnp.float32)], axis=1)

    def solve_wells(rate):
        totals = jnp.zeros((per_owner + 1,), jnp.float32).at[targets].add(rate)
        seg_rate = jnp.einsum(
            "wgh,wh->wg",
            well_inverse,
            totals[:per_owner].reshape(well_count, seg_count),
            precision=lax.Precision.HIGHEST,
        )
        padded = jnp.concatenate([seg_rate.reshape(-1), jnp.zeros((1,), jnp.float32)])
        return padded[targets]

    def well_term(vector):
        flattened = vector.reshape(layers, comps, tile_area)
        values = flattened[layer_idx, :, column_idx]
        outgoing = jnp.moveaxis(values, 2, 0)
        arrived = lax.all_to_all(outgoing, ("gx", "gy"), split_axis=1, concat_axis=1, tiled=True)
        coeff_in = pad_in[:, targets]
        rate = coeff_in[0] * arrived[0] + coeff_in[1] * arrived[1] + coeff_in[2] * arrived[2]
        back = solve_wells(rate)
        terms = lax.all_to_all(
            pad_out[:, targets] * back[None], ("gx", "gy"), split_axis=1, concat_axis=1, tiled=True
        )
        scattered = (
            jnp.zeros((layers, comps, tile_area), jnp.float32)
            .at[layer_idx, :, column_idx]
            .add(jnp.moveaxis(terms, 0, 2))
        )
        return scattered.reshape(vector.shape)

    def apply_operator(vector):
        flux = couple(mobility, vector)
        extended = padded_2(flux, (("gx", 2), ("gy", 3)), 1)
        return stencil(vector, extended, diag_block, face_trans) - well_term(vector)

    iterate = first_guess
    residual = right_side - apply_operator(iterate)
    shadow = residual
    inner_now = lax.psum(jnp.sum(shadow * residual), ("gx", "gy"))
    search = residual
    for iteration in range(ITERS):
        search_hat = precondition(search, column_inverse)
        applied = apply_operator(search_hat)
        projected = lax.psum(jnp.sum(shadow * applied), ("gx", "gy"))
        step_size = inner_now / projected
        halfway = residual - step_size * applied
        halfway_hat = precondition(halfway, column_inverse)
        response = apply_operator(halfway_hat)
        cross_term, self_term, shadow_term = lax.psum(
            (jnp.sum(response * halfway), jnp.sum(response * response), jnp.sum(shadow * response)),
            ("gx", "gy"),
        )
        smoothing = cross_term / self_term
        iterate = iterate + step_size * search_hat + smoothing * halfway_hat
        residual = halfway - smoothing * response
        if iteration + 1 < ITERS:
            inner_next = inner_now - step_size * projected - smoothing * shadow_term
            momentum = inner_next / inner_now * (step_size / smoothing)
            search = residual + momentum * (search - smoothing * applied)
            inner_now = inner_next
    return (iterate, right_side - apply_operator(iterate))


def solution(mesh):
    in_specs = (
        P(None, None, "gx", "gy"),
        P(None, None, "gx", "gy"),
        P(None, None, None, "gx", "gy"),
        P(None, None, None, "gx", "gy"),
        P(None, None, "gx", "gy"),
        P(None, None, None, "gx", "gy"),
        P(("gx", "gy"), None, None),
        P(("gx", "gy"), None, None),
        P(None, ("gx", "gy")),
        P(None, ("gx", "gy")),
        P(("gx", "gy"), None, None),
    )
    out_specs = (P(None, None, "gx", "gy"), P(None, None, "gx", "gy"))
    return jax.shard_map(
        per_device, mesh=mesh, in_specs=in_specs, out_specs=out_specs, check_vma=False
    )
```

profile of v0, /device:TPU:0, one launch (start us, length us, event | category | flops | bytes accessed | tf_op | source)
XLA Modules:
  0.0 752.7 jit_solution(8360309148296932770)
XLA Ops:
  1.6 5.7 copy.372
  7.4 9.6 %gather_fusion.2 = f32[1280,3]{1,0:T(8,128)S(1)} fusion(f32[8,3,2048]{1,2,0:T(8,128)} %bitcast.585, s32[1280]{0:T(1024)S(1)} %reshape.496), kind=kCustom, calls=%fused_computation.2 | custom fusion | bytes 40960 | tf_op jit(solution)/shard_map/gather | solution.py:94
  17.9 7.3 all-to-all-start
  49.9 8.4 %scatter_custom_fusion = f32[1025]{0:T(1024)S(1)} fusion(s32[1280]{0:T(1024)S(1)} %reshape.482, f32[1280]{0:T(1024)S(1)} %reshape.584, f32[]{:T(128)} %constant.32.clone.1), kind=kCustom, calls=%fused_computation.405 | custom fusion | flops 1280 | bytes 4104 | tf_op jit(solution)/shard_map/scatter-add | solution.py:82
  59.3 7.1 gather_fusion.3
  67.2 5.3 all-to-all-start.1
  73.1 6.7 all-to-all-done.1
  81.0 13.1 %scatter_custom_fusion.6 = f32[3,16384]{0,1:T(8,128)} fusion(s32[1280]{0:T(1024)S(1)} %reshape.628, f32[1280,3]{1,0:T(8,128)} %bitcast.636, f32[]{:T(128)} %constant.32.clone.1), kind=kCustom, calls=%fused_computation.36 | custom fusion | flops 3840 | bytes 197120
  94.1 5.9 copy.377
  106.4 5.1 collective-permute-start.4
  113.0 5.6 copy.398
  118.6 12.7 %gather_fusion.4 = f32[1280,3]{1,0:T(8,128)} fusion(f32[8,3,2048]{1,2,0:T(8,128)} %copy.398, s32[1280]{0:T(1024)S(1)} %reshape.496), kind=kCustom, calls=%fused_computation.4 | custom fusion | bytes 40960 | tf_op jit(solution)/shard_map/gather | solution.py:94
  147.1 8.6 %scatter_custom_fusion.1 = f32[1025]{0:T(1024)S(1)} fusion(s32[1280]{0:T(1024)} %copy-done.66, f32[1280]{0:T(1024)} %reshape.592, f32[]{:T(128)} %constant.32.clone.1), kind=kCustom, calls=%fused_computation.403 | custom fusion | flops 1280 | bytes 4612 | tf_op jit(solution)/shard_map/scatter-add | solution.py:82
  156.6 10.0 %gather_fusion.5 = f32[1280]{0:T(1024)} fusion(f32[1025]{0:T(1024)S(1)} %pad_maximum_fusion.58, s32[2048]{0:T(1024)} %copy-done.22), kind=kCustom, calls=%fused_computation.5 | custom fusion | bytes 15360 | tf_op jit(solution)/shard_map/gather | solution.py:90
  176.3 5.6 all-to-all-done.3
  183.9 12.9 %scatter_custom_fusion.7 = f32[3,16384]{0,1:T(8,128)} fusion(s32[1280]{0:T(1024)} %copy-done.70, f32[1280,3]{1,0:T(8,128)} %bitcast.637, f32[]{:T(128)} %constant.32.clone.1), kind=kCustom, calls=%fused_computation.34 | custom fusion | flops 3840 | bytes 197120
  196.8 5.9 copy.403
  206.3 38.8 %all-reduce.16 = (f32[]{:T(128)}, f32[]{:T(128)}) all-reduce(f32[]{:T(128)} %get-tuple-element.18, f32[]{:T(128)} %get-tuple-element.17), channel_id=1, replica_groups=mesh['gx'=4,'gy'=8] {'gx','gy'}, use_global_device_ids=true, to_apply=%region_3.4 | all-reduce | flops 2 | bytes 16 | tf_op jit(solution)/shard_map/psum | solution.py:118
  252.3 5.4 collective-permute-start.8
  259.1 5.6 copy.418
  264.7 12.7 %gather_fusion.6 = f32[1280,3]{1,0:T(8,128)} fusion(f32[8,3,2048]{1,2,0:T(8,128)} %copy.418, s32[1280]{0:T(1024)S(1)} %reshape.496), kind=kCustom, calls=%fused_computation.6 | custom fusion | bytes 40960 | tf_op jit(solution)/shard_map/gather | solution.py:94
  293.8 8.6 %scatter_custom_fusion.2 = f32[1025]{0:T(1024)S(1)} fusion(s32[1280]{0:T(1024)} %copy-done.66, f32[1280]{0:T(1024)} %reshape.600, f32[]{:T(128)} %constant.32.clone.1), kind=kCustom, calls=%fused_computation.401 | custom fusion | flops 1280 | bytes 4612 | tf_op jit(solution)/shard_map/scatter-add | solution.py:82
  303.3 10.0 %gather_fusion.7 = f32[1280]{0:T(1024)} fusion(f32[1025]{0:T(1024)S(1)} %pad_maximum_fusion.57, s32[2048]{0:T(1024)} %copy-done.22), kind=kCustom, calls=%fused_computation.7 | custom fusion | bytes 15360 | tf_op jit(solution)/shard_map/gather | solution.py:90
  330.4 12.9 %scatter_custom_fusion.8 = f32[3,16384]{0,1:T(8,128)} fusion(s32[1280]{0:T(1024)} %copy-done.70, f32[1280,3]{1,0:T(8,128)} %bitcast.638, f32[]{:T(128)} %constant.32.clone.1), kind=kCustom, calls=%fused_computation.32 | custom fusion | flops 3840 | bytes 197120
  343.4 5.9 copy.423
  352.9 38.6 %all-reduce.15 = (f32[]{:T(128)}, f32[]{:T(128)}, f32[]{:T(128)}) all-reduce(f32[]{:T(128)} %get-tuple-element.16, f32[]{:T(128)} %get-tuple-element.15, f32[]{:T(128)} %get-tuple-element.14), channel_id=1, replica_groups=mesh['gx'=4,'gy'=8] {'gx','gy'}, use_global_device_ids=true, to_apply=%region_11.12 | all-reduce | flops 3 | bytes 24 | tf_op jit(solution)/shard_map/psum | solution.py:128
  402.1 5.4 collective-permute-start.12
  408.9 5.6 copy.437
  414.5 12.7 %gather_fusion.8 = f32[1280,3]{1,0:T(8,128)} fusion(f32[8,3,2048]{1,2,0:T(8,128)} %copy.437, s32[1280]{0:T(1024)S(1)} %reshape.496), kind=kCustom, calls=%fused_computation.8 | custom fusion | bytes 40960 | tf_op jit(solution)/shard_map/gather | solution.py:94
  443.4 8.6 %scatter_custom_fusion.3 = f32[1025]{0:T(1024)S(1)} fusion(s32[1280]{0:T(1024)} %copy-done.66, f32[1280]{0:T(1024)} %reshape.608, f32[]{:T(128)} %constant.32.clone.1), kind=kCustom, calls=%fused_computation.399 | custom fusion | flops 1280 | bytes 4612 | tf_op jit(solution)/shard_map/scatter-add | solution.py:82
  453.0 10.0 %gather_fusion.9 = f32[1280]{0:T(1024)} fusion(f32[1025]{0:T(1024)S(1)} %pad_maximum_fusion.56, s32[2048]{0:T(1024)} %copy-done.22), kind=kCustom, calls=%fused_computation.9 | custom fusion | bytes 15360 | tf_op jit(solution)/shard_map/gather | solution.py:90
  472.7 5.6 all-to-all-done.7
  480.3 12.9 %scatter_custom_fusion.9 = f32[3,16384]{0,1:T(8,128)} fusion(s32[1280]{0:T(1024)} %copy-done.70, f32[1280,3]{1,0:T(8,128)} %bitcast.639, f32[]{:T(128)} %constant.32.clone.1), kind=kCustom, calls=%fused_computation.30 | custom fusion | flops 3840 | bytes 197120
  493.2 5.9 copy.442
  502.5 38.4 %psum.61 = f32[]{:T(128)} all-reduce(f32[]{:T(128)} %get-tuple-element.26), channel_id=1, replica_groups=mesh['gx'=4,'gy'=8] {'gx','gy'}, use_global_device_ids=true, to_apply=%region_19.20 | all-reduce | flops 1 | bytes 8 | tf_op jit(solution)/shard_map/psum | solution.py:123
  556.5 9.6 %gather_fusion.10 = f32[1280,3]{1,0:T(8,128)S(1)} fusion(f32[8,3,2048]{1,2,0:T(8,128)} %copy.456, s32[1280]{0:T(1024)S(1)} %reshape.496), kind=kCustom, calls=%fused_computation.10 | custom fusion | bytes 40960 | tf_op jit(solution)/shard_map/gather | solution.py:94
  578.9 8.6 %scatter_custom_fusion.4 = f32[1025]{0:T(1024)S(1)} fusion(s32[1280]{0:T(1024)} %copy-done.66, f32[1280]{0:T(1024)S(1)} %reshape.616, f32[]{:T(128)} %constant.32.clone.1), kind=kCustom, calls=%fused_computation.397 | custom fusion | flops 1280 | bytes 4612 | tf_op jit(solution)/shard_map/scatter-add | solution.py:82
  588.5 7.1 gather_fusion.11
  601.0 6.7 all-to-all-done.9
  609.0 12.9 %scatter_custom_fusion.10 = f32[3,16384]{0,1:T(8,128)} fusion(s32[1280]{0:T(1024)} %copy-done.70, f32[1280,3]{1,0:T(8,128)} %bitcast.640, f32[]{:T(128)} %constant.32.clone.1), kind=kCustom, calls=%fused_computation.28 | custom fusion | flops 3840 | bytes 197120
  621.9 5.3 copy.461
  629.5 38.6 %all-reduce.14 = (f32[]{:T(128)}, f32[]{:T(128)}) all-reduce(f32[]{:T(128)} %get-tuple-element.13, f32[]{:T(128)} %get-tuple-element.12), channel_id=1, replica_groups=mesh['gx'=4,'gy'=8] {'gx','gy'}, use_global_device_ids=true, to_apply=%region_23.24 | all-reduce | flops 2 | bytes 16 | tf_op jit(solution)/shard_map/psum | solution.py:128
  680.5 9.6 %gather_fusion.12 = f32[1280,3]{1,0:T(8,128)S(1)} fusion(f32[8,3,2048]{1,2,0:T(8,128)} %bitcast.586, s32[1280]{0:T(1024)S(1)} %reshape.496), kind=kCustom, calls=%fused_computation.12 | custom fusion | bytes 40960 | tf_op jit(solution)/shard_map/gather | solution.py:94
  703.0 8.6 %scatter_custom_fusion.5 = f32[1025]{0:T(1024)S(1)} fusion(s32[1280]{0:T(1024)} %copy-done.66, f32[1280]{0:T(1024)S(1)} %reshape.624, f32[]{:T(128)} %constant.32.clone.1), kind=kCustom, calls=%fused_computation.395 | custom fusion | flops 1280 | bytes 4612 | tf_op jit(solution)/shard_map/scatter-add | solution.py:82
  712.6 7.1 gather_fusion.13
  725.0 6.7 all-to-all-done.11
  732.0 12.8 %scatter_custom_fusion.11 = f32[3,16384]{0,1:T(8,128)} fusion(s32[1280]{0:T(1024)} %copy-done.70, f32[1280,3]{1,0:T(8,128)S(1)} %bitcast.635, f32[]{:T(128)} %constant.32.clone.1), kind=kCustom, calls=%fused_computation.26 | custom fusion | flops 3840 | bytes 197120
  744.8 5.2 copy.467
  (401 shorter events, 221.4 us)
Async XLA Ops:
  0.6 57.7 %copy-start = (f32[8,128,128]{2,1,0:T(8,128)S(1)}, f32[8,128,128]{2,1,0:T(8,128)}, u32[]{:S(2)}) copy-start(f32[8,128,128]{2,1,0:T(8,128)} %param.21) | copy-start | bytes 1572868
  17.9 31.8 %all-to-all-start = ((f32[3,32,40]{2,0,1:T(4,128)}), f32[3,32,40]{2,0,1:T(4,128)S(1)}, u32[]{:S(2)}, u32[]{:S(2)}) async-start(f32[3,32,40]{2,0,1:T(4,128)} %bitcast.22), calls=%async_computation | async-start | bytes 131072 | tf_op jit(solution)/shard_map/all_to_all | solution.py:96
  25.4 33.9 %copy-start.11 = (f32[8,3,16,128]{3,2,0,1:T(8,128)}, f32[8,3,16,128]{3,2,0,1:T(8,128)S(1)}, u32[]{:S(2)}) copy-start(f32[8,3,16,128]{3,2,0,1:T(8,128)S(1)} %fusion.39) | copy-start | bytes 589828
  25.4 18.2 %collective-permute-start.1 = (f32[8,3,1,128]{3,2,0,1:T(1,128)S(1)}, f32[8,3,1,128]{3,2,0,1:T(1,128)S(1)}, u32[]{:S(2)}, u32[]{:S(2)}) collective-permute-start(f32[8,3,1,128]{3,2,0,1:T(1,128)S(1)} %get-tuple-element.122), channel_id=1, source_target_pairs={{8,0},{16,8},{24,16},{9,1},{17,9},{25,17},{10,2},{18,10},{26,18},{... | collective-permute-start | bytes 36872 | tf_op jit(solution)/shard_map/ppermute | solution.py:17
  26.7 16.9 %collective-permute-start = (f32[8,3,1,128]{3,2,0,1:T(1,128)S(1)}, f32[8,3,1,128]{3,2,0,1:T(1,128)S(1)}, u32[]{:S(2)}, u32[]{:S(2)}) collective-permute-start(f32[8,3,1,128]{3,2,0,1:T(1,128)S(1)} %get-tuple-element.121), channel_id=1, source_target_pairs={{0,8},{8,16},{16,24},{1,9},{9,17},{17,25},{2,10},{10,18},{18,26},{... | collective-permute-start | bytes 36872 | tf_op jit(solution)/shard_map/ppermute | solution.py:14
  32.5 33.9 %copy-start.66 = (s32[1280]{0:T(1024)}, s32[1280]{0:T(1024)S(1)}, u32[]{:S(2)}) copy-start(s32[1280]{0:T(1024)S(1)} %reshape.482) | copy-start | bytes 15364
  44.6 55.4 %collective-permute-start.3 = (f32[8,3,18,1]{3,2,0,1:T(8,128)}, f32[8,3,18,1]{3,2,0,1:T(8,128)}, u32[]{:S(2)}, u32[]{:S(2)}) collective-permute-start(f32[8,3,18,1]{3,2,0,1:T(8,128)} %get-tuple-element.56), channel_id=1, source_target_pairs={{1,0},{2,1},{3,2},{4,3},{5,4},{6,5},{7,6},{9,8},{10,9},{11,10},{12... | collective-permute-start | bytes 5192 | tf_op jit(solution)/shard_map/ppermute | solution.py:17
  45.9 54.1 %collective-permute-start.2 = (f32[8,3,18,1]{3,2,0,1:T(8,128)}, f32[8,3,18,1]{3,2,0,1:T(8,128)}, u32[]{:S(2)}, u32[]{:S(2)}) collective-permute-start(f32[8,3,18,1]{3,2,0,1:T(8,128)} %get-tuple-element.55), channel_id=1, source_target_pairs={{0,1},{1,2},{2,3},{3,4},{4,5},{5,6},{6,7},{8,9},{9,10},{10,11},{11... | collective-permute-start | bytes 5192 | tf_op jit(solution)/shard_map/ppermute | solution.py:14
  67.2 12.7 %all-to-all-start.1 = ((f32[3,32,40]{2,0,1:T(4,128)}), f32[3,32,40]{2,0,1:T(4,128)S(1)}, u32[]{:S(2)}, u32[]{:S(2)}) async-start(f32[3,32,40]{2,0,1:T(4,128)} %multiply_bitcast_fusion.5), calls=%async_computation.1 | async-start | bytes 131072 | tf_op jit(solution)/shard_map/all_to_all | solution.py:100
  105.1 31.6 %collective-permute-start.5 = (f32[8,3,1,128]{3,2,0,1:T(1,128)}, f32[8,3,1,128]{3,2,0,1:T(1,128)}, u32[]{:S(2)}, u32[]{:S(2)}) collective-permute-start(f32[8,3,1,128]{3,2,0,1:T(1,128)} %get-tuple-element.107), channel_id=1, source_target_pairs={{8,0},{16,8},{24,16},{9,1},{17,9},{25,17},{10,2},{18,10},{26,18},{... | collective-permute-start | bytes 36872 | tf_op jit(solution)/shard_map/ppermute | solution.py:17
  106.4 30.3 %collective-permute-start.4 = (f32[8,3,1,128]{3,2,0,1:T(1,128)}, f32[8,3,1,128]{3,2,0,1:T(1,128)}, u32[]{:S(2)}, u32[]{:S(2)}) collective-permute-start(f32[8,3,1,128]{3,2,0,1:T(1,128)} %get-tuple-element.106), channel_id=1, source_target_pairs={{0,8},{8,16},{16,24},{1,9},{9,17},{17,25},{2,10},{10,18},{18,26},{... | collective-permute-start | bytes 36872 | tf_op jit(solution)/shard_map/ppermute | solution.py:14
  133.4 10.5 %all-to-all-start.2 = ((f32[3,32,40]{2,0,1:T(4,128)}), f32[3,32,40]{2,0,1:T(4,128)}, u32[]{:S(2)}, u32[]{:S(2)}) async-start(f32[3,32,40]{2,0,1:T(4,128)} %bitcast.707), calls=%async_computation.2 | async-start | bytes 131072 | tf_op jit(solution)/shard_map/all_to_all | solution.py:96
  138.6 64.1 %collective-permute-start.7 = (f32[8,3,18,1]{3,2,0,1:T(8,128)}, f32[8,3,18,1]{3,2,0,1:T(8,128)}, u32[]{:S(2)}, u32[]{:S(2)}) collective-permute-start(f32[8,3,18,1]{3,2,0,1:T(8,128)} %get-tuple-element.51), channel_id=1, source_target_pairs={{1,0},{2,1},{3,2},{4,3},{5,4},{6,5},{7,6},{9,8},{10,9},{11,10},{12... | collective-permute-start | bytes 5192 | tf_op jit(solution)/shard_map/ppermute | solution.py:17
  139.9 62.8 %collective-permute-start.6 = (f32[8,3,18,1]{3,2,0,1:T(8,128)}, f32[8,3,18,1]{3,2,0,1:T(8,128)}, u32[]{:S(2)}, u32[]{:S(2)}) collective-permute-start(f32[8,3,18,1]{3,2,0,1:T(8,128)} %get-tuple-element.50), channel_id=1, source_target_pairs={{0,1},{1,2},{2,3},{3,4},{4,5},{5,6},{6,7},{8,9},{9,10},{10,11},{11... | collective-permute-start | bytes 5192 | tf_op jit(solution)/shard_map/ppermute | solution.py:14
  169.5 12.4 %all-to-all-start.3 = ((f32[3,32,40]{2,0,1:T(4,128)}), f32[3,32,40]{2,0,1:T(4,128)}, u32[]{:S(2)}, u32[]{:S(2)}) async-start(f32[3,32,40]{2,0,1:T(4,128)} %multiply_bitcast_fusion.4), calls=%async_computation.3 | async-start | bytes 131072 | tf_op jit(solution)/shard_map/all_to_all | solution.py:100
  251.0 32.4 %collective-permute-start.9 = (f32[8,3,1,128]{3,2,0,1:T(1,128)}, f32[8,3,1,128]{3,2,0,1:T(1,128)}, u32[]{:S(2)}, u32[]{:S(2)}) collective-permute-start(f32[8,3,1,128]{3,2,0,1:T(1,128)} %get-tuple-element.94), channel_id=1, source_target_pairs={{8,0},{16,8},{24,16},{9,1},{17,9},{25,17},{10,2},{18,10},{26,18},{... | collective-permute-start | bytes 36872 | tf_op jit(solution)/shard_map/ppermute | solution.py:17
  252.3 31.1 %collective-permute-start.8 = (f32[8,3,1,128]{3,2,0,1:T(1,128)}, f32[8,3,1,128]{3,2,0,1:T(1,128)}, u32[]{:S(2)}, u32[]{:S(2)}) collective-permute-start(f32[8,3,1,128]{3,2,0,1:T(1,128)} %get-tuple-element.93), channel_id=1, source_target_pairs={{0,8},{8,16},{16,24},{1,9},{9,17},{17,25},{2,10},{10,18},{18,26},{... | collective-permute-start | bytes 36872 | tf_op jit(solution)/shard_map/ppermute | solution.py:14
  279.4 11.2 %all-to-all-start.4 = ((f32[3,32,40]{2,0,1:T(4,128)}), f32[3,32,40]{2,0,1:T(4,128)}, u32[]{:S(2)}, u32[]{:S(2)}) async-start(f32[3,32,40]{2,0,1:T(4,128)} %bitcast.708), calls=%async_computation.4 | async-start | bytes 131072 | tf_op jit(solution)/shard_map/all_to_all | solution.py:96
  285.3 64.0 %collective-permute-start.11 = (f32[8,3,18,1]{3,2,0,1:T(8,128)}, f32[8,3,18,1]{3,2,0,1:T(8,128)}, u32[]{:S(2)}, u32[]{:S(2)}) collective-permute-start(f32[8,3,18,1]{3,2,0,1:T(8,128)} %get-tuple-element.49), channel_id=1, source_target_pairs={{1,0},{2,1},{3,2},{4,3},{5,4},{6,5},{7,6},{9,8},{10,9},{11,10},{12... | collective-permute-start | bytes 5192 | tf_op jit(solution)/shard_map/ppermute | solution.py:17
  286.6 62.7 %collective-permute-start.10 = (f32[8,3,18,1]{3,2,0,1:T(8,128)}, f32[8,3,18,1]{3,2,0,1:T(8,128)}, u32[]{:S(2)}, u32[]{:S(2)}) collective-permute-start(f32[8,3,18,1]{3,2,0,1:T(8,128)} %get-tuple-element.48), channel_id=1, source_target_pairs={{0,1},{1,2},{2,3},{3,4},{4,5},{5,6},{6,7},{8,9},{9,10},{10,11},{11... | collective-permute-start | bytes 5192 | tf_op jit(solution)/shard_map/ppermute | solution.py:14
  316.2 12.3 %all-to-all-start.5 = ((f32[3,32,40]{2,0,1:T(4,128)}), f32[3,32,40]{2,0,1:T(4,128)}, u32[]{:S(2)}, u32[]{:S(2)}) async-start(f32[3,32,40]{2,0,1:T(4,128)} %multiply_bitcast_fusion.3), calls=%async_computation.5 | async-start | bytes 131072 | tf_op jit(solution)/shard_map/all_to_all | solution.py:100
  400.8 32.3 %collective-permute-start.13 = (f32[8,3,1,128]{3,2,0,1:T(1,128)}, f32[8,3,1,128]{3,2,0,1:T(1,128)}, u32[]{:S(2)}, u32[]{:S(2)}) collective-permute-start(f32[8,3,1,128]{3,2,0,1:T(1,128)} %get-tuple-element.81), channel_id=1, source_target_pairs={{8,0},{16,8},{24,16},{9,1},{17,9},{25,17},{10,2},{18,10},{26,18},{... | collective-permute-start | bytes 36872 | tf_op jit(solution)/shard_map/ppermute | solution.py:17
  402.1 31.0 %collective-permute-start.12 = (f32[8,3,1,128]{3,2,0,1:T(1,128)}, f32[8,3,1,128]{3,2,0,1:T(1,128)}, u32[]{:S(2)}, u32[]{:S(2)}) collective-permute-start(f32[8,3,1,128]{3,2,0,1:T(1,128)} %get-tuple-element.80), channel_id=1, source_target_pairs={{0,8},{8,16},{16,24},{1,9},{9,17},{17,25},{2,10},{10,18},{18,26},{... | collective-permute-start | bytes 36872 | tf_op jit(solution)/shard_map/ppermute | solution.py:14
  429.2 11.1 %all-to-all-start.6 = ((f32[3,32,40]{2,0,1:T(4,128)}), f32[3,32,40]{2,0,1:T(4,128)}, u32[]{:S(2)}, u32[]{:S(2)}) async-start(f32[3,32,40]{2,0,1:T(4,128)} %bitcast.709), calls=%async_computation.6 | async-start | bytes 131072 | tf_op jit(solution)/shard_map/all_to_all | solution.py:96
  435.0 64.0 %collective-permute-start.15 = (f32[8,3,18,1]{3,2,0,1:T(8,128)}, f32[8,3,18,1]{3,2,0,1:T(8,128)}, u32[]{:S(2)}, u32[]{:S(2)}) collective-permute-start(f32[8,3,18,1]{3,2,0,1:T(8,128)} %get-tuple-element.47), channel_id=1, source_target_pairs={{1,0},{2,1},{3,2},{4,3},{5,4},{6,5},{7,6},{9,8},{10,9},{11,10},{12... | collective-permute-start | bytes 5192 | tf_op jit(solution)/shard_map/ppermute | solution.py:17
  436.3 62.7 %collective-permute-start.14 = (f32[8,3,18,1]{3,2,0,1:T(8,128)}, f32[8,3,18,1]{3,2,0,1:T(8,128)}, u32[]{:S(2)}, u32[]{:S(2)}) collective-permute-start(f32[8,3,18,1]{3,2,0,1:T(8,128)} %get-tuple-element.46), channel_id=1, source_target_pairs={{0,1},{1,2},{2,3},{3,4},{4,5},{5,6},{6,7},{8,9},{9,10},{10,11},{11... | collective-permute-start | bytes 5192 | tf_op jit(solution)/shard_map/ppermute | solution.py:14
  465.8 12.4 %all-to-all-start.7 = ((f32[3,32,40]{2,0,1:T(4,128)}), f32[3,32,40]{2,0,1:T(4,128)}, u32[]{:S(2)}, u32[]{:S(2)}) async-start(f32[3,32,40]{2,0,1:T(4,128)} %multiply_bitcast_fusion.2), calls=%async_computation.7 | async-start | bytes 131072 | tf_op jit(solution)/shard_map/all_to_all | solution.py:100
  544.9 26.5 %collective-permute-start.17 = (f32[8,3,1,128]{3,2,0,1:T(1,128)S(1)}, f32[8,3,1,128]{3,2,0,1:T(1,128)S(1)}, u32[]{:S(2)}, u32[]{:S(2)}) collective-permute-start(f32[8,3,1,128]{3,2,0,1:T(1,128)S(1)} %get-tuple-element.70), channel_id=1, source_target_pairs={{8,0},{16,8},{24,16},{9,1},{17,9},{25,17},{10,2},{18,10},{26,18},{... | collective-permute-start | bytes 36872 | tf_op jit(solution)/shard_map/ppermute | solution.py:17
  546.2 25.2 %collective-permute-start.16 = (f32[8,3,1,128]{3,2,0,1:T(1,128)S(1)}, f32[8,3,1,128]{3,2,0,1:T(1,128)S(1)}, u32[]{:S(2)}, u32[]{:S(2)}) collective-permute-start(f32[8,3,1,128]{3,2,0,1:T(1,128)S(1)} %get-tuple-element.69), channel_id=1, source_target_pairs={{0,8},{8,16},{16,24},{1,9},{9,17},{17,25},{2,10},{10,18},{18,26},{... | collective-permute-start | bytes 36872 | tf_op jit(solution)/shard_map/ppermute | solution.py:14
  551.7 36.7 %copy-start.23 = (s32[2048]{0:T(1024)S(1)}, s32[2048]{0:T(1024)}, u32[]{:S(2)}) copy-start(s32[2048]{0:T(1024)} %copy-done.22) | copy-start | bytes 24580
  567.0 11.8 %all-to-all-start.8 = ((f32[3,32,40]{2,0,1:T(4,128)}), f32[3,32,40]{2,0,1:T(4,128)S(1)}, u32[]{:S(2)}, u32[]{:S(2)}) async-start(f32[3,32,40]{2,0,1:T(4,128)} %bitcast.150), calls=%async_computation.8 | async-start | bytes 131072 | tf_op jit(solution)/shard_map/all_to_all | solution.py:96
  572.4 54.8 %collective-permute-start.19 = (f32[8,3,18,1]{3,2,0,1:T(8,128)}, f32[8,3,18,1]{3,2,0,1:T(8,128)}, u32[]{:S(2)}, u32[]{:S(2)}) collective-permute-start(f32[8,3,18,1]{3,2,0,1:T(8,128)} %get-tuple-element.45), channel_id=1, source_target_pairs={{1,0},{2,1},{3,2},{4,3},{5,4},{6,5},{7,6},{9,8},{10,9},{11,10},{12... | collective-permute-start | bytes 5192 | tf_op jit(solution)/shard_map/ppermute | solution.py:17
  573.7 53.5 %collective-permute-start.18 = (f32[8,3,18,1]{3,2,0,1:T(8,128)}, f32[8,3,18,1]{3,2,0,1:T(8,128)}, u32[]{:S(2)}, u32[]{:S(2)}) collective-permute-start(f32[8,3,18,1]{3,2,0,1:T(8,128)} %get-tuple-element.44), channel_id=1, source_target_pairs={{0,1},{1,2},{2,3},{3,4},{4,5},{5,6},{6,7},{8,9},{9,10},{10,11},{11... | collective-permute-start | bytes 5192 | tf_op jit(solution)/shard_map/ppermute | solution.py:14
  596.3 11.3 %all-to-all-start.9 = ((f32[3,32,40]{2,0,1:T(4,128)}), f32[3,32,40]{2,0,1:T(4,128)S(1)}, u32[]{:S(2)}, u32[]{:S(2)}) async-start(f32[3,32,40]{2,0,1:T(4,128)} %multiply_bitcast_fusion.1), calls=%async_computation.9 | async-start | bytes 131072 | tf_op jit(solution)/shard_map/all_to_all | solution.py:100
  608.9 60.6 %copy-start.27 = (f32[8,3,16,128]{3,2,0,1:T(8,128)S(1)}, f32[8,3,16,128]{3,2,0,1:T(8,128)}, u32[]{:S(2)}) copy-start(f32[8,3,16,128]{3,2,0,1:T(8,128)} %copy-done.26) | copy-start | bytes 589828
  608.9 60.6 %copy-start.29 = (f32[8,3,16,128]{3,2,0,1:T(8,128)S(1)}, f32[8,3,16,128]{3,2,0,1:T(8,128)}, u32[]{:S(2)}) copy-start(f32[8,3,16,128]{3,2,0,1:T(8,128)} %copy-done.28) | copy-start | bytes 589828
  608.9 60.6 %copy-start.31 = (f32[8,3,16,128]{3,2,0,1:T(8,128)S(1)}, f32[8,3,16,128]{3,2,0,1:T(8,128)}, u32[]{:S(2)}) copy-start(f32[8,3,16,128]{3,2,0,1:T(8,128)} %copy-done.30) | copy-start | bytes 589828
  608.9 60.6 %copy-start.33 = (f32[8,3,16,128]{3,2,0,1:T(8,128)S(1)}, f32[8,3,16,128]{3,2,0,1:T(8,128)}, u32[]{:S(2)}) copy-start(f32[8,3,16,128]{3,2,0,1:T(8,128)} %copy-done.32) | copy-start | bytes 589828
  608.9 60.6 %copy-start.37 = (f32[8,3,16,128]{3,2,1,0:T(8,128)S(1)}, f32[8,3,16,128]{3,2,1,0:T(8,128)}, u32[]{:S(2)}) copy-start(f32[8,3,16,128]{3,2,1,0:T(8,128)} %param.12) | copy-start | bytes 589828
  621.9 47.7 %copy-start.6 = (bf16[8,3,1,16,128]{4,3,2,1,0:T(8,128)(2,1)S(1)}, bf16[8,3,1,16,128]{4,3,2,1,0:T(8,128)(2,1)}, u32[]{:S(2)}) copy-start(bf16[8,3,1,16,128]{4,3,2,1,0:T(8,128)(2,1)} %copy-done.5) | copy-start | bytes 294916
  621.9 47.7 %copy-start.8 = (bf16[8,3,1,16,128]{4,3,2,1,0:T(8,128)(2,1)S(1)}, bf16[8,3,1,16,128]{4,3,2,1,0:T(8,128)(2,1)}, u32[]{:S(2)}) copy-start(bf16[8,3,1,16,128]{4,3,2,1,0:T(8,128)(2,1)} %copy-done.7) | copy-start | bytes 294916
  621.9 47.8 %copy-start.10 = (bf16[8,3,1,16,128]{4,3,2,1,0:T(8,128)(2,1)S(1)}, bf16[8,3,1,16,128]{4,3,2,1,0:T(8,128)(2,1)}, u32[]{:S(2)}) copy-start(bf16[8,3,1,16,128]{4,3,2,1,0:T(8,128)(2,1)} %copy-done.9) | copy-start | bytes 294916
  669.8 25.7 %collective-permute-start.21 = (f32[8,3,1,128]{3,2,0,1:T(1,128)S(1)}, f32[8,3,1,128]{3,2,0,1:T(1,128)S(1)}, u32[]{:S(2)}, u32[]{:S(2)}) collective-permute-start(f32[8,3,1,128]{3,2,0,1:T(1,128)S(1)} %get-tuple-element.63), channel_id=1, source_target_pairs={{8,0},{16,8},{24,16},{9,1},{17,9},{25,17},{10,2},{18,10},{26,18},{... | collective-permute-start | bytes 36872 | tf_op jit(solution)/shard_map/ppermute | solution.py:17
  671.1 24.4 %collective-permute-start.20 = (f32[8,3,1,128]{3,2,0,1:T(1,128)S(1)}, f32[8,3,1,128]{3,2,0,1:T(1,128)S(1)}, u32[]{:S(2)}, u32[]{:S(2)}) collective-permute-start(f32[8,3,1,128]{3,2,0,1:T(1,128)S(1)} %get-tuple-element.62), channel_id=1, source_target_pairs={{0,8},{8,16},{16,24},{1,9},{9,17},{17,25},{2,10},{10,18},{18,26},{... | collective-permute-start | bytes 36872 | tf_op jit(solution)/shard_map/ppermute | solution.py:14
  691.0 11.8 %all-to-all-start.10 = ((f32[3,32,40]{2,0,1:T(4,128)}), f32[3,32,40]{2,0,1:T(4,128)S(1)}, u32[]{:S(2)}, u32[]{:S(2)}) async-start(f32[3,32,40]{2,0,1:T(4,128)} %bitcast.167), calls=%async_computation.10 | async-start | bytes 131072 | tf_op jit(solution)/shard_map/all_to_all | solution.py:96
  696.4 53.6 %collective-permute-start.23 = (f32[8,3,18,1]{3,2,0,1:T(8,128)}, f32[8,3,18,1]{3,2,0,1:T(8,128)}, u32[]{:S(2)}, u32[]{:S(2)}) collective-permute-start(f32[8,3,18,1]{3,2,0,1:T(8,128)} %get-tuple-element.43), channel_id=1, source_target_pairs={{1,0},{2,1},{3,2},{4,3},{5,4},{6,5},{7,6},{9,8},{10,9},{11,10},{12... | collective-permute-start | bytes 5192 | tf_op jit(solution)/shard_map/ppermute | solution.py:17
  697.7 52.3 %collective-permute-start.22 = (f32[8,3,18,1]{3,2,0,1:T(8,128)}, f32[8,3,18,1]{3,2,0,1:T(8,128)}, u32[]{:S(2)}, u32[]{:S(2)}) collective-permute-start(f32[8,3,18,1]{3,2,0,1:T(8,128)} %get-tuple-element.42), channel_id=1, source_target_pairs={{0,1},{1,2},{2,3},{3,4},{4,5},{5,6},{6,7},{8,9},{9,10},{10,11},{11... | collective-permute-start | bytes 5192 | tf_op jit(solution)/shard_map/ppermute | solution.py:14
  720.4 11.2 %all-to-all-start.11 = ((f32[3,32,40]{2,0,1:T(4,128)}), f32[3,32,40]{2,0,1:T(4,128)S(1)}, u32[]{:S(2)}, u32[]{:S(2)}) async-start(f32[3,32,40]{2,0,1:T(4,128)} %multiply_bitcast_fusion), calls=%async_computation.11 | async-start | bytes 131072 | tf_op jit(solution)/shard_map/all_to_all | solution.py:100
  (61 other events, 909.2 us)
where the time goes:
time: 763 us; the launch traced here: 753 us
  local copies, waits for them, and re-layouts  242 us (32%)
  other arithmetic  175 us (23%)
  blocking collectives  154 us (20%)
  starting transfers between devices  124 us (16%)
  waiting for transfers between devices  38.7 us (5%)
  between operations  13.2 us (2%)
    unnamed x9, other arithmetic  77.9 us
    psum x2, blocking collectives, per_device(): lax.psum((jnp.sum(response * halfway), jnp.sum(response * response), jnp....  77.2 us
    gather x12, local copies, waits for them, and re-layouts, well_term(): values = flattened[layer_idx, :, column_idx]  75.7 us
    gather x12, local copies, waits for them, and re-layouts, solve_wells(): return padded[targets]  55.7 us
    ppermute x12, starting transfers between devices, padded_2(): lax.ppermute(lax.slice_in_dim(block, block.shape[dim] - width, None, axis...  52.9 us
    scatter-add x6, other arithmetic, solve_wells(): totals = jnp.zeros((per_owner + 1,), jnp.float32).at[targets].add(rate)  51.4 us
    unnamed x176, local copies, waits for them, and re-layouts  45.4 us
    psum x1, blocking collectives, per_device(): inner_now = lax.psum(jnp.sum(shadow * residual), ('gx', 'gy'))  38.8 us
  transfers between devices with their start and end apart: 36, of which 11 were waited for; matrix products, arithmetic and copies ran while one was open for 50% of the time, Pallas kernels for 0%

commit v1 on v0

v1 whole, which is shorter than its diff:
```python
import functools

import jax
import jax.numpy as jnp
from jax import lax
from jax.experimental import pallas as pl
from jax.experimental.pallas import tpu as pltpu
from jax.sharding import PartitionSpec as P

ITERS = 2
AXES = ("gx", "gy")
LANES = 128
SUBS = 8
F32 = jnp.float32
BF16 = jnp.bfloat16
SCOPED = 16 * 1024 * 1024


class Geometry:
    def __init__(self, vector_shape, table_shape, inverse_shape, n_gy):
        self.layers, self.comps, self.rows, self.cols = vector_shape
        self.devices, self.cap = table_shape
        self.wells, self.segs = inverse_shape[:2]
        self.n_gy = n_gy
        self.tile_rows = self.layers * self.rows
        self.faces = self.layers * self.comps
        self.per = LANES // self.cap
        self.groups = -(-self.devices // self.per)
        self.groups_pad = -(-self.groups // SUBS) * SUBS
        self.vector = (self.layers, self.comps, self.rows, self.cols)
        self.padded = (self.faces, self.rows + 2 * SUBS, self.cols)
        assert self.cols == LANES and self.segs == LANES and self.rows == 2 * SUBS
        assert self.faces + SUBS <= self.devices and 2 * self.faces <= LANES
        assert 3 * self.cap <= LANES

    def pieces(self):
        for k in range(self.per):
            low = k * self.groups
            count = min(self.groups, self.devices - low)
            if count > 0:
                yield k, low, count


def call(body, outs, args, scratch=()):
    spec = pl.BlockSpec(memory_space=pltpu.VMEM)
    held = [pltpu.with_memory_space_constraint(a, pltpu.VMEM) for a in args]
    return pl.pallas_call(
        body,
        out_shape=tuple(pltpu.VMEM(shape, dtype) for shape, dtype in outs),
        in_specs=[spec] * len(held),
        out_specs=(spec,) * len(outs),
        scratch_shapes=list(scratch),
        compiler_params=pltpu.CompilerParams(vmem_limit_bytes=SCOPED),
    )(*held)


def iota(shape, dim):
    return lax.broadcasted_iota(jnp.int32, shape, dim)


def take_lanes(table, index):
    return jnp.take_along_axis(table, index, axis=1, mode="promise_in_bounds")


def spread(row, shape):
    return jnp.broadcast_to(row, shape)


def total(block):
    return jnp.sum(jnp.sum(block, axis=0, keepdims=True), axis=1, keepdims=True)


def pack_slots(geo, block_ref, lane, packed_ref):
    packed_ref[...] = jnp.zeros_like(packed_ref)
    start = lane // LANES * LANES
    for k, low, count in geo.pieces():
        part = block_ref[low : low + count, start : start + LANES]
        shift = (k * geo.cap - lane) % LANES
        part = pltpu.roll(part, shift, 1) if shift else part
        at = iota(part.shape, 1)
        mine = (at >= k * geo.cap) & (at < (k + 1) * geo.cap)
        packed_ref[0:count, :] = jnp.where(mine, part, packed_ref[0:count, :])


def unpack_slots(geo, packed, lane, block_ref):
    for k, low, count in geo.pieces():
        shift = (lane - k * geo.cap) % LANES
        part = pltpu.roll(packed, shift, 1) if shift else packed
        part = part[0:count]
        at = iota(part.shape, 1)
        mine = (at >= lane) & (at < lane + geo.cap)
        block_ref[low : low + count, 0:LANES] = jnp.where(
            mine, part, block_ref[low : low + count, 0:LANES]
        )


def setup_body(geo, cell_ref, slot_ref, inverse_ref, rowp, lanep, row_hot, lane_hot, hi, lo, inv_dev, inv_pos, turned, wide, packed):
    shape = (geo.devices, LANES)
    wide[...] = jnp.zeros_like(wide)
    wide[:, 0 : geo.cap] = cell_ref[...] + 1
    pack_slots(geo, wide, 0, packed)
    cells = packed[...] - 1
    row = cells >> 7
    lane = cells & (LANES - 1)
    rowp[...] = row
    lanep[...] = lane
    for g in range(geo.groups):
        here = slice(g * LANES, (g + 1) * LANES)
        rows = spread(row[g : g + 1], (geo.tile_rows, LANES))
        row_hot[:, here] = jnp.where(rows == iota(rows.shape, 0), 1.0, 0.0).astype(BF16)
        lanes = spread(lane[g : g + 1], (LANES, LANES))
        lane_hot[:, here] = jnp.where(lanes == iota(lanes.shape, 0), 1.0, 0.0).astype(BF16)
    wide[:, 0 : geo.cap] = slot_ref[...] + 1
    slots = wide[...] - 1
    hi[...] = slots >> 7
    lo[...] = slots & (LANES - 1)
    pack_slots(geo, wide, 0, packed)
    slots = packed[...] - 1
    slot_hi = slots >> 7
    slot_lo = slots & (LANES - 1)
    at = iota((geo.wells, LANES), 1)
    piece = lax.div(at, geo.cap)
    position = (lax.rem(at, geo.cap) + 1).astype(F32)
    found = jnp.zeros((2 * geo.wells, LANES), F32)
    for g in range(geo.groups):
        well = spread(slot_hi[g : g + 1], (geo.wells, LANES)) == iota((geo.wells, LANES), 0)
        device = (piece * geo.groups + (g + 1)).astype(F32)
        marks = jnp.concatenate([jnp.where(well, device, 0.0), jnp.where(well, position, 0.0)], axis=0)
        segs = spread(slot_lo[g : g + 1], (LANES, LANES))
        hot = jnp.where(segs == iota(segs.shape, 0), 1.0, 0.0).astype(BF16)
        found += lax.dot_general(marks.astype(BF16), hot, (((1,), (1,)), ((), ())), preferred_element_type=F32)
    inv_dev[...] = found[: geo.wells].astype(jnp.int32) - 1
    inv_pos[...] = jnp.maximum(found[geo.wells :].astype(jnp.int32) - 1, 0)
    for w in range(geo.wells):
        turned[w] = inverse_ref[w].T


def write_faces(geo, flux, send):
    one, two, three = LANES, 2 * LANES, 3 * LANES
    if geo.devices > geo.faces + SUBS:
        send[geo.faces + SUBS :, one:three] = jnp.zeros((geo.devices - geo.faces - SUBS, 2 * LANES), F32)
    at = iota((geo.rows, LANES), 1)
    edges = jnp.zeros((geo.rows, LANES), F32)
    for j in range(geo.faces):
        block = flux[j, SUBS : SUBS + geo.rows, :]
        send[j : j + 1, one:two] = flux[j, SUBS : SUBS + 1, :]
        send[j : j + 1, two:three] = flux[j, SUBS + geo.rows - 1 : SUBS + geo.rows, :]
        turned = pltpu.roll(block, 2 * j + 1, 1)
        edges = jnp.where((at >> 1) == j, turned, edges)
    send[geo.faces : geo.faces + SUBS, one:two] = edges[:SUBS]
    send[geo.faces : geo.faces + SUBS, two:three] = edges[SUBS:]


def write_flux(geo, mobility, vector, flux):
    for z in range(geo.layers):
        v = [vector[z, b] for b in range(3)]
        for a in range(3):
            block = mobility[z, a, 0].astype(F32) * v[0]
            block += mobility[z, a, 1].astype(F32) * v[1]
            block += mobility[z, a, 2].astype(F32) * v[2]
            flux[3 * z + a, SUBS : SUBS + geo.rows, :] = block


def gather_cells(geo, vector, rowp, lanep, finish):
    shape = (SUBS, LANES)
    for g in range(geo.groups):
        lane = spread(lanep[g : g + 1, :], shape)
        row = spread(rowp[g : g + 1, :], shape) - iota(shape, 0)
        kept = [jnp.zeros(shape, F32) for _ in range(3)]
        for z in range(geo.layers):
            for h in range(geo.rows // SUBS):
                mine = row == z * geo.rows + h * SUBS
                for c in range(3):
                    found = take_lanes(vector[z, c, h * SUBS : (h + 1) * SUBS, :], lane)
                    kept[c] = jnp.where(mine, found, kept[c])
        finish(g, kept)


def precondition(geo, inverse, source, target):
    for h in range(geo.layers // 2):
        v = [source[2 * h + f // 3, f % 3] for f in range(6)]
        for e in range(6):
            block = inverse[h, e, 0].astype(F32) * v[0]
            for f in range(1, 6):
                block += inverse[h, e, f].astype(F32) * v[f]
            target[2 * h + e // 3, e % 3] = block


def first_body(geo, guess, mobility, rowp, lanep, flux, send, packed):
    write_flux(geo, mobility, guess, flux)
    write_faces(geo, flux, send)
    send[:, 0:LANES] = jnp.zeros((geo.devices, LANES), F32)
    packed[...] = jnp.zeros_like(packed)

    def finish(g, kept):
        for c in range(3):
            packed[c, g : g + 1, :] = jnp.sum(kept[c], axis=0, keepdims=True)

    gather_cells(geo, guess, rowp, lanep, finish)
    for c in range(3):
        unpack_slots(geo, packed[c], c * geo.cap, send)


def relay(geo, me, came, back):
    shape = (geo.devices, LANES)
    at = iota(shape, 0)
    even = (iota(shape, 1) & 1) == 0
    within = lax.rem(at, geo.n_gy)
    faces = me[0:1, :] < geo.faces
    up, down, count = geo.n_gy, geo.devices - geo.n_gy, geo.devices
    one = came[:, LANES : 2 * LANES]
    two = came[:, 2 * LANES : 3 * LANES]
    after = jnp.where(at < down, pltpu.roll(one, down, 0), 0.0)
    before = jnp.where(at >= up, pltpu.roll(two, up, 0), 0.0)

    def beside(block):
        low = jnp.where(within > 0, pltpu.roll(block, 1, 0), 0.0)
        high = jnp.where(within < geo.n_gy - 1, pltpu.roll(block, count - 1, 0), 0.0)
        return jnp.where(even, low, high)

    faces = spread(faces, shape)
    back[:, LANES : 2 * LANES] = jnp.where(faces, after, beside(one))
    back[:, 2 * LANES : 3 * LANES] = jnp.where(faces, before, beside(two))


def at_segments(geo, came, inv_dev, inv_pos, offset):
    shape = (geo.wells, LANES)
    device = inv_dev[...]
    position = inv_pos[...] + offset
    kept = jnp.zeros(shape, F32)
    for s in range(geo.devices):
        found = take_lanes(spread(came[s : s + 1, 0:LANES], shape), position)
        kept = jnp.where(device == s, found, kept)
    return kept


def at_slots(geo, rows, hi, lo):
    shape = (geo.devices, LANES)
    kept = jnp.zeros(shape, F32)
    for w in range(geo.wells):
        found = take_lanes(spread(rows[w], shape), lo)
        kept = jnp.where(hi == w, found, kept)
    return kept


def solve_segments(geo, rate, turned):
    rate_t = rate.T
    rows = []
    for w in range(geo.wells):
        rows.append(jnp.sum(turned[w] * rate_t[:, w : w + 1], axis=0, keepdims=True))
    return rows


def owner_first_body(geo, came, me, inv_dev, inv_pos, hi_ref, lo_ref, turned, well_in, well_out, back):
    shape = (geo.wells, LANES)
    hi, lo = hi_ref[...], lo_ref[...]
    rate = jnp.zeros(shape, F32)
    rows_in = [[well_in[c : c + 1, w * LANES : (w + 1) * LANES] for w in range(geo.wells)] for c in range(3)]
    rows_out = [[well_out[c : c + 1, w * LANES : (w + 1) * LANES] for w in range(geo.wells)] for c in range(3)]
    for c in range(3):
        rate += jnp.concatenate(rows_in[c], axis=0) * at_segments(geo, came, inv_dev, inv_pos, c * geo.cap)
    back[:, 0:LANES] = at_slots(geo, solve_segments(geo, rate, turned), hi, lo)
    relay(geo, me, came, back)
    for place, rows in ((3, rows_in), (4, rows_out)):
        block = jnp.zeros((geo.devices, LANES), F32)
        for c in range(3):
            part = at_slots(geo, rows[c], hi, lo)
            block += pltpu.roll(part, c * geo.cap, 1) if c else part
        back[:, place * LANES : (place + 1) * LANES] = block


def owner_body(geo, came, me, inv_dev, inv_pos, hi_ref, lo_ref, turned, back, sums):
    rate = at_segments(geo, came, inv_dev, inv_pos, 0)
    back[:, 0:LANES] = at_slots(geo, solve_segments(geo, rate, turned), hi_ref[...], lo_ref[...])
    relay(geo, me, came, back)
    sums[...] = spread(jnp.sum(came[:, 0:LANES], axis=0, keepdims=True), sums.shape)


def scatter_terms(geo, came, coeff_out, row_hot, lane_hot, packed, spots):
    pack_slots(geo, came, 0, packed)
    width = geo.groups * LANES
    sum_of = None
    parts = []
    for c in range(3):
        value = coeff_out[c] * packed[...]
        high = value.astype(BF16)
        rest = value - high.astype(F32)
        middle = rest.astype(BF16)
        low = (rest - middle.astype(F32)).astype(BF16)
        parts.append((high, middle, low))
    result = None
    for g in range(geo.groups):
        here = slice(g * LANES, (g + 1) * LANES)
        hot = row_hot[:, here]
        left = jnp.concatenate(
            [hot * spread(parts[c][k][g : g + 1], hot.shape) for c in range(3) for k in range(3)], axis=0
        )
        piece = lax.dot_general(left, lane_hot[:, here], (((1,), (1,)), ((), ())), preferred_element_type=F32)
        result = piece if result is None else result + piece
    n = geo.tile_rows
    for c in range(3):
        base = 3 * c * n
        spots[c * n : (c + 1) * n, :] = (
            result[base : base + n] + result[base + n : base + 2 * n] + result[base + 2 * n : base + 3 * n]
        )


def apply_operator(geo, came, vector, flux, diag, face, spots, store):
    shape = (geo.rows, LANES)
    at_row, at_lane = iota(shape, 0), iota(shape, 1)
    one, two, three = LANES, 2 * LANES, 3 * LANES
    edges = jnp.concatenate(
        [came[geo.faces : geo.faces + SUBS, one:two], came[geo.faces : geo.faces + SUBS, two:three]], axis=0
    )
    inside = slice(SUBS, SUBS + geo.rows)
    for z in range(geo.layers):
        f = [face[n, z].astype(F32) for n in range(6)]
        v = [vector[z, b] for b in range(3)]
        for a in range(3):
            j = 3 * z + a
            block = flux[j, inside, :]
            under = jnp.where(at_row == 0, spread(came[j : j + 1, two:three], shape), flux[j, SUBS - 1 : SUBS - 1 + geo.rows, :])
            over = jnp.where(at_row == geo.rows - 1, spread(came[j : j + 1, one:two], shape), flux[j, SUBS + 1 : SUBS + 1 + geo.rows, :])
            left = jnp.where(at_lane == 0, spread(edges[:, 2 * j : 2 * j + 1], shape), pltpu.roll(block, 1, 1))
            right = jnp.where(at_lane == LANES - 1, spread(edges[:, 2 * j + 1 : 2 * j + 2], shape), pltpu.roll(block, LANES - 1, 1))
            beside = f[0] * under + f[1] * over + f[2] * left + f[3] * right
            if z > 0:
                beside += f[4] * flux[j - 3, inside, :]
            if z + 1 < geo.layers:
                beside += f[5] * flux[j + 3, inside, :]
            own = diag[z, a, 0].astype(F32) * v[0]
            own += diag[z, a, 1].astype(F32) * v[1]
            own += diag[z, a, 2].astype(F32) * v[2]
            base = a * geo.tile_rows + z * geo.rows
            store(z, a, own - beside - spots[base : base + geo.rows, :])


def send_next(geo, source, inverse, mobility, rowp, lanep, coeff_in, dots, ahead, flux, send, packed):
    precondition(geo, inverse, source, ahead)
    write_flux(geo, mobility, ahead, flux)
    write_faces(geo, flux, send)
    at = iota((1, LANES), 1)
    row = jnp.zeros((1, LANES), F32)
    for n, dot in enumerate(dots):
        row = jnp.where(at == geo.cap + n, spread(total(dot), (1, LANES)), row)
    send[:, 0:LANES] = spread(row, (geo.devices, LANES))
    packed[...] = jnp.zeros_like(packed)

    def finish(g, kept):
        rate = kept[0] * spread(coeff_in[0, g : g + 1, :], kept[0].shape)
        rate += kept[1] * spread(coeff_in[1, g : g + 1, :], kept[0].shape)
        rate += kept[2] * spread(coeff_in[2, g : g + 1, :], kept[0].shape)
        packed[g : g + 1, :] = jnp.sum(rate, axis=0, keepdims=True)

    gather_cells(geo, ahead, rowp, lanep, finish)
    unpack_slots(geo, packed[...], 0, send)


def each_tile(geo):
    for z in range(geo.layers):
        for c in range(geo.comps):
            yield z, c


COMMON = 8


def stage_zero_body(geo, came, guess, flux_in, diag, face, row_hot, lane_hot, inverse, mobility, rowp, lanep, right_side,
                    shadow, coeff_in, coeff_out, ahead, flux, send, packed, spots):
    for c in range(3):
        pack_slots(geo, came, 3 * LANES + c * geo.cap, packed)
        coeff_in[c] = packed[...]
        pack_slots(geo, came, 4 * LANES + c * geo.cap, packed)
        coeff_out[c] = packed[...]
    scatter_terms(geo, came, coeff_out, row_hot, lane_hot, packed, spots)
    dots = [jnp.zeros((geo.rows, LANES), F32)]

    def store(z, c, image):
        value = right_side[z, c] - image
        shadow[z, c] = value
        dots[0] += value * value

    apply_operator(geo, came, guess, flux_in, diag, face, spots, store)
    send_next(geo, shadow, inverse, mobility, rowp, lanep, coeff_in, dots, ahead, flux, send, packed)


def stage_image_body(geo, came, vector, flux_in, diag, face, row_hot, lane_hot, inverse, mobility, rowp, lanep, coeff_in, coeff_out, shadow,
                     image_out, ahead, flux, send, packed, spots):
    scatter_terms(geo, came, coeff_out, row_hot, lane_hot, packed, spots)
    dots = [jnp.zeros((geo.rows, LANES), F32)]

    def store(z, c, image):
        image_out[z, c] = image
        dots[0] += shadow[z, c] * image

    apply_operator(geo, came, vector, flux_in, diag, face, spots, store)
    send_next(geo, image_out, inverse, mobility, rowp, lanep, coeff_in, dots, ahead, flux, send, packed)


def stage_half_body(geo, came, vector, flux_in, diag, face, row_hot, lane_hot, inverse, mobility, rowp, lanep, coeff_in, coeff_out, shadow,
                    step, residual, applied, behind,
                    deeper, half, response, ahead, flux, send, packed, spots):
    scatter_terms(geo, came, coeff_out, row_hot, lane_hot, packed, spots)
    dots = [jnp.zeros((geo.rows, LANES), F32) for _ in range(4)]
    scale = spread(step[0:1, 0:1], (geo.rows, LANES))

    def store(z, c, image):
        deeper[z, c] = image
        s = residual[z, c] - scale * applied[z, c]
        t = behind[z, c] - scale * image
        half[z, c] = s
        response[z, c] = t
        dots[0] += t * s
        dots[1] += t * t
        dots[2] += shadow[z, c] * t
        dots[3] += shadow[z, c] * s

    apply_operator(geo, came, vector, flux_in, diag, face, spots, store)
    send_next(geo, response, inverse, mobility, rowp, lanep, coeff_in, dots, ahead, flux, send, packed)


def stage_next_body(geo, came, vector, flux_in, diag, face, row_hot, lane_hot, inverse, mobility, rowp, lanep, coeff_in, coeff_out, shadow,
                    smoothing, momentum, half, response, applied, deeper,
                    residual_out, behind_out, applied_out, ahead, flux, send, packed, spots):
    scatter_terms(geo, came, coeff_out, row_hot, lane_hot, packed, spots)
    dots = [jnp.zeros((geo.rows, LANES), F32)]
    smooth = spread(smoothing[0:1, 0:1], (geo.rows, LANES))
    keep = spread(momentum[0:1, 0:1], (geo.rows, LANES))

    def store(z, c, image):
        t = response[z, c]
        residual_out[z, c] = half[z, c] - smooth * t
        w = t - smooth * image
        behind_out[z, c] = w
        v = w + keep * (applied[z, c] - smooth * deeper[z, c])
        applied_out[z, c] = v
        dots[0] += shadow[z, c] * v

    apply_operator(geo, came, vector, flux_in, diag, face, spots, store)
    send_next(geo, applied_out, inverse, mobility, rowp, lanep, coeff_in, dots, ahead, flux, send, packed)


def stage_last_body(geo, came, vector, flux_in, diag, face, row_hot, lane_hot, coeff_out, step, residual, applied, behind,
                    half, response, send, packed, spots):
    scatter_terms(geo, came, coeff_out, row_hot, lane_hot, packed, spots)
    dots = [jnp.zeros((geo.rows, LANES), F32) for _ in range(2)]
    scale = spread(step[0:1, 0:1], (geo.rows, LANES))

    def store(z, c, image):
        s = residual[z, c] - scale * applied[z, c]
        t = behind[z, c] - scale * image
        half[z, c] = s
        response[z, c] = t
        dots[0] += t * s
        dots[1] += t * t

    apply_operator(geo, came, vector, flux_in, diag, face, spots, store)
    at = iota((1, LANES), 1)
    row = jnp.where(at == 0, spread(total(dots[0]), (1, LANES)), spread(total(dots[1]), (1, LANES)))
    send[...] = spread(row, send.shape)


def pick(sums, geo, n):
    return sums[:, geo.cap + n : geo.cap + n + 1]


def ratio_body(geo, upper, sums, step):
    step[...] = spread(upper[:, 0:1] / pick(sums, geo, 0), step.shape)


def scalars_body(geo, sums, rho, step, smoothing, momentum, rho_out):
    smooth = pick(sums, geo, 0) / pick(sums, geo, 1)
    rho_next = pick(sums, geo, 3) - smooth * pick(sums, geo, 2)
    smoothing[...] = spread(smooth, smoothing.shape)
    momentum[...] = spread((rho_next / rho[:, 0:1]) * (step[:, 0:1] / smooth), momentum.shape)
    rho_out[...] = spread(rho_next, rho_out.shape)


def rho_body(geo, sums, rho):
    rho[...] = spread(pick(sums, geo, 0), rho.shape)


def update_body(geo, step, smoothing, momentum, iterate, search_hat, applied_hat, residual_hat, response_hat,
                iterate_out, residual_out, search_out):
    shape = (geo.rows, LANES)
    alpha, omega, beta = (spread(x[0:1, 0:1], shape) for x in (step, smoothing, momentum))
    for z, c in each_tile(geo):
        half_hat = residual_hat[z, c] - alpha * applied_hat[z, c]
        iterate_out[z, c] = iterate[z, c] + alpha * search_hat[z, c] + omega * half_hat
        next_hat = half_hat - omega * response_hat[z, c]
        residual_out[z, c] = next_hat
        search_out[z, c] = next_hat + beta * (search_hat[z, c] - omega * applied_hat[z, c])


def ready_body(geo, step, iterate, search_hat, residual_hat, applied_hat, iterate_out, half_out):
    alpha = spread(step[0:1, 0:1], (geo.rows, LANES))
    for z, c in each_tile(geo):
        iterate_out[z, c] = iterate[z, c] + alpha * search_hat[z, c]
        half_out[z, c] = residual_hat[z, c] - alpha * applied_hat[z, c]


def finish_body(geo, came, iterate, half_hat, half, response, solution_out, residual_out):
    sums = jnp.sum(came[...], axis=0, keepdims=True)
    omega = spread(sums[:, 0:1] / sums[:, 1:2], (geo.rows, LANES))
    for z, c in each_tile(geo):
        solution_out[z, c] = iterate[z, c] + omega * half_hat[z, c]
        residual_out[z, c] = half[z, c] - omega * response[z, c]


def exchange(rows):
    return lax.all_to_all(rows, AXES, split_axis=0, concat_axis=0, tiled=True)


def per_device(right_side, guess, diag, mobility, face, inverse, perf_cell, perf_slot, well_in, well_out, well_inverse):
    geo = Geometry(right_side.shape, perf_cell.shape[1:], well_inverse.shape, lax.axis_size("gy"))
    bind = lambda body: functools.partial(body, geo)
    me = jnp.broadcast_to(lax.axis_index(AXES), (SUBS, LANES)).astype(jnp.int32)
    block = (geo.devices, LANES)
    packed_shape = (geo.groups_pad, LANES)
    wide = (geo.devices, 3 * LANES)
    seg_shape = (geo.wells, LANES)
    small = ((SUBS, LANES), F32)
    vec = (geo.vector, F32)
    hot = geo.groups * LANES
    ints = jnp.int32
    rowp, lanep, row_hot, lane_hot, hi, lo, inv_dev, inv_pos, turned = call(
        bind(setup_body),
        [(packed_shape, ints), (packed_shape, ints), ((geo.tile_rows, hot), BF16), ((LANES, hot), BF16), (block, ints), (block, ints),
         (seg_shape, ints), (seg_shape, ints), (well_inverse.shape, F32)],
        [perf_cell[0], perf_slot[0], well_inverse],
        [pltpu.VMEM(block, ints), pltpu.VMEM(packed_shape, ints)],
    )
    owner_tables = [me, inv_dev, inv_pos, hi, lo, turned]
    packed = pltpu.VMEM(packed_shape, F32)
    spots = pltpu.VMEM((3 * geo.tile_rows, LANES), F32)
    coeffs = ((3,) + packed_shape, F32)
    sent = [vec, (geo.padded, F32), (wide, F32)]

    flux, send = call(
        bind(first_body), [(geo.padded, F32), (wide, F32)], [guess, mobility, rowp, lanep], [pltpu.VMEM((3,) + packed_shape, F32)]
    )
    (back,) = call(bind(owner_first_body), [((geo.devices, 5 * LANES), F32)], [exchange(send)] + owner_tables + [well_in, well_out])
    shadow, coeff_in, coeff_out, ahead, flux, send = call(
        bind(stage_zero_body), [vec, coeffs, coeffs] + sent,
        [exchange(back), guess, flux, diag, face, row_hot, lane_hot, inverse, mobility, rowp, lanep, right_side], [packed, spots],
    )
    hats = [diag, face, row_hot, lane_hot, inverse, mobility, rowp, lanep, coeff_in, coeff_out, shadow]

    def owner(send):
        back, sums = call(bind(owner_body), [(wide, F32), small], [exchange(send)] + owner_tables)
        return exchange(back), sums

    came, sums = owner(send)
    (rho,) = call(bind(rho_body), [small], [sums])
    search_hat = residual_hat = ahead
    applied, ahead, flux, send = call(
        bind(stage_image_body), [vec] + sent, [came, ahead, flux] + hats, [packed, spots]
    )
    residual, behind, iterate = shadow, applied, guess
    for iteration in range(ITERS):
        applied_hat = ahead
        came, sums = owner(send)
        (step,) = call(bind(ratio_body), [small], [rho, sums])
        if iteration + 1 == ITERS:
            half, response, send = call(
                bind(stage_last_body), [vec, vec, (block, F32)],
                [came, ahead, flux, diag, face, row_hot, lane_hot, coeff_out, step, residual, applied, behind], [packed, spots],
            )
            break
        deeper, half, response, ahead, flux, send = call(
            bind(stage_half_body), [vec, vec, vec] + sent, [came, ahead, flux] + hats + [step, residual, applied, behind], [packed, spots]
        )
        response_hat = ahead
        came, sums = owner(send)
        smoothing, momentum, rho = call(bind(scalars_body), [small] * 3, [sums, rho, step])
        residual, behind, applied, ahead, flux, send = call(
            bind(stage_next_body), [vec, vec, vec] + sent,
            [came, ahead, flux] + hats + [smoothing, momentum, half, response, applied, deeper], [packed, spots],
        )
        iterate, residual_hat, search_hat = call(
            bind(update_body), [vec] * 3, [step, smoothing, momentum, iterate, search_hat, applied_hat, residual_hat, response_hat]
        )
    iterate, half_hat = call(bind(ready_body), [vec] * 2, [step, iterate, search_hat, residual_hat, applied_hat])
    return call(bind(finish_body), [vec] * 2, [exchange(send), iterate, half_hat, half, response])


def solution(mesh):
    in_specs = (
        P(None, None, "gx", "gy"),
        P(None, None, "gx", "gy"),
        P(None, None, None, "gx", "gy"),
        P(None, None, None, "gx", "gy"),
        P(None, None, "gx", "gy"),
        P(None, None, None, "gx", "gy"),
        P(AXES, None, None),
        P(AXES, None, None),
        P(None, AXES),
        P(None, AXES),
        P(AXES, None, None),
    )
    out_specs = (P(None, None, "gx", "gy"), P(None, None, "gx", "gy"))
    return jax.shard_map(per_device, mesh=mesh, in_specs=in_specs, out_specs=out_specs, check_vma=False)
```

time: 763 us -> 149 us (0.20); the launches traced: 753 us -> 148 us
  local copies, waits for them, and re-layouts: 242 us -> 21.4 us
  other arithmetic: 175 us -> 0 us
  starting transfers between devices: 124 us -> 19.1 us
  blocking collectives: 154 us -> 54.4 us
  Pallas kernels: 0 us -> 16.8 us
  between operations: 13.2 us -> 1.03 us
    psum x4 -> x0, blocking collectives: 154 us -> none  [the longest x2 77.2 us: per_device(): lax.psum((jnp.sum(response * halfway), jnp.sum(response * response), jnp....]
    gather x28 -> x0, local copies, waits for them, and re-layouts: 140 us -> none  [the longest x12 75.7 us: well_term(): values = flattened[layer_idx, :, column_idx]]
    unnamed x9 -> x0, other arithmetic: 77.9 us -> none
    ppermute x24 -> x0, starting transfers between devices: 68.3 us -> none  [the longest x12 52.9 us: padded_2(): lax.ppermute(lax.slice_in_dim(block, block.shape[dim] - width, None, axis...]
    all_to_all x0 -> x6, blocking collectives: none -> 54.4 us  [exchange(): return lax.all_to_all(rows, AXES, split_axis=0, concat_axis=0, tiled=True)]
    scatter-add x6 -> x0, other arithmetic: 51.4 us -> none  [solve_wells(): totals = jnp.zeros((per_owner + 1,), jnp.float32).at[targets].add(rate)]
    all_to_all x12 -> x5, starting transfers between devices: 55.4 us -> 19.1 us  [exchange(): return lax.all_to_all(rows, AXES, split_axis=0, concat_axis=0, tiled=True)]
    add x12 -> x0, local copies, waits for them, and re-layouts: 30.7 us -> none  [the longest x4 21.5 us: precondition(): result + column_inverse[:, :, member].astype(jnp.float32) * paired[:, mem...]
  transfers between devices with their start and end apart: 36 -> 5, of which waited for: 11 -> 5; matrix products, arithmetic and copies ran while one was open for 50% -> 0% of each run, Pallas kernels for 0% -> 1%
where the time goes in v1:
time: 149 us; the launch traced here: 148 us
  blocking collectives  54.4 us (37%)
  waiting for transfers between devices  35.3 us (24%)
  local copies, waits for them, and re-layouts  21.4 us (14%)
  starting transfers between devices  19.1 us (13%)
  Pallas kernels  16.8 us (11%)
    all_to_all x6, blocking collectives, exchange(): return lax.all_to_all(rows, AXES, split_axis=0, concat_axis=0, tiled=True)  54.4 us
    all_to_all x5, waiting for transfers between devices, exchange(): return lax.all_to_all(rows, AXES, split_axis=0, concat_axis=0, tiled=True)  35.3 us
    all_to_all x5, starting transfers between devices, exchange(): return lax.all_to_all(rows, AXES, split_axis=0, concat_axis=0, tiled=True)  19.1 us
    unnamed x90, local copies, waits for them, and re-layouts  18.3 us
    pallas_call x19, Pallas kernels, call(): pl.pallas_call(body, out_shape=tuple((pltpu.VMEM(shape, dtype) for shape,...  16.8 us
    all_to_all x10, local copies, waits for them, and re-layouts, exchange(): return lax.all_to_all(rows, AXES, split_axis=0, concat_axis=0, tiled=True)  3.12 us
  transfers between devices with their start and end apart: 5, of which 5 were waited for; matrix products, arithmetic and copies ran while one was open for 0% of the time, Pallas kernels for 1%

profile of v1, /device:TPU:0, one launch (start us, length us, event | category | flops | bytes accessed | tf_op | source)
XLA Modules:
  0.0 148.1 jit_solution(11934599254441757844)
XLA Ops:
  0.7 1.1 copy-done.13
  1.7 0.7 copy-done.35
  2.4 0.7 copy-done.36
  4.1 0.8 shard_map.123
  4.9 0.8 copy.13
  5.7 7.3 %all-to-all-start = ((f32[32,1,384]{2,1,0:T(1,128)}), f32[32,1,384]{2,1,0:T(1,128)S(1)}, u32[]{:S(2)}, u32[]{:S(2)}) async-start(f32[32,1,384]{2,1,0:T(1,128)} %copy.13), calls=%async_computation | async-start | bytes 98304 | tf_op jit(solution)/shard_map/all_to_all | solution.py:511
  13.0 7.3 %all-to-all-done = f32[32,1,384]{2,1,0:T(1,128)S(1)} async-done(((f32[32,1,384]{2,1,0:T(1,128)}), f32[32,1,384]{2,1,0:T(1,128)S(1)}, u32[]{:S(2)}, u32[]{:S(2)}) %all-to-all-start) | async-done | bytes 49184 | tf_op jit(solution)/shard_map/all_to_all | solution.py:511
  20.4 1.4 shard_map.124
  21.9 9.4 %all_to_all.121 = f32[32,1,640]{2,1,0:T(1,128)S(1)} all-to-all(f32[32,1,640]{2,1,0:T(1,128)S(1)} %copy.14), channel_id=1, replica_groups=mesh['gx'=4,'gy'=8] {'gx','gy'}, dimensions={0} | all-to-all | bytes 163840 | tf_op jit(solution)/shard_map/all_to_all | solution.py:511
  31.3 1.0 copy-done.17
  32.3 2.3 %shard_map.125 = (f32[8,3,16,128]{3,2,1,0:T(8,128)S(1)}, f32[3,16,128]{2,1,0:T(8,128)S(1)}, f32[3,16,128]{2,1,0:T(8,128)S(1)}, f32[8,3,16,128]{3,2,1,0:T(8,128)S...) custom-call(f32[32,640]{1,0:T(8,128)S(1)} %bitcast.46, f32[8,3,16,128]{3,2,1,0:T(8,128)S(1)} %copy-done.4, ...), custom_call_target="tpu_custom_call" | custom-call | tf_op jit(solution)/shard_map/pallas_call | solution.py:47
  34.7 9.0 %all_to_all.122 = f32[32,1,384]{2,1,0:T(1,128)S(1)} all-to-all(f32[32,1,384]{2,1,0:T(1,128)S(1)} %copy.15), channel_id=1, replica_groups=mesh['gx'=4,'gy'=8] {'gx','gy'}, dimensions={0} | all-to-all | bytes 98304 | tf_op jit(solution)/shard_map/all_to_all | solution.py:511
  44.3 9.0 %all_to_all.123 = f32[32,1,384]{2,1,0:T(1,128)S(1)} all-to-all(f32[32,1,384]{2,1,0:T(1,128)S(1)} %copy.16), channel_id=1, replica_groups=mesh['gx'=4,'gy'=8] {'gx','gy'}, dimensions={0} | all-to-all | bytes 98304 | tf_op jit(solution)/shard_map/all_to_all | solution.py:511
  53.3 2.2 %shard_map.127 = (f32[8,3,16,128]{3,2,1,0:T(8,128)S(1)}, f32[8,3,16,128]{3,2,1,0:T(8,128)S(1)}, f32[24,32,128]{2,1,0:T(8,128)S(1)}, f32[32,384]{1,0:T(8,128)S(1)}) custom-call(f32[32,384]{1,0:T(8,128)S(1)} %bitcast.55, f32[8,3,16,128]{3,2,1,0:T(8,128)S(1)} %get-tuple-element.67.vector.search_hat.residual_hat, f32[24,32,128]{2,1,0:T(8,128)S(1)} %get-tuple-element.68.flux_in, ...), custom_call_target="tpu_custom_call" | custom-call | tf_op jit(solution)/shard_map/pallas_call | solution.py:47
  55.6 9.0 %all_to_all.124 = f32[32,1,384]{2,1,0:T(1,128)S(1)} all-to-all(f32[32,1,384]{2,1,0:T(1,128)S(1)} %copy.17), channel_id=1, replica_groups=mesh['gx'=4,'gy'=8] {'gx','gy'}, dimensions={0} | all-to-all | bytes 98304 | tf_op jit(solution)/shard_map/all_to_all | solution.py:511
  65.2 0.7 copy.18
  65.8 3.3 %all-to-all-start.5 = ((f32[32,1,384]{2,1,0:T(1,128)}), f32[32,1,384]{2,1,0:T(1,128)}, u32[]{:S(2)}, u32[]{:S(2)}) async-start(f32[32,1,384]{2,1,0:T(1,128)} %copy.18), calls=%async_computation.5 | async-start | bytes 98304 | tf_op jit(solution)/shard_map/all_to_all | solution.py:511
  69.3 7.1 %all-to-all-done.5 = f32[32,1,384]{2,1,0:T(1,128)} async-done(((f32[32,1,384]{2,1,0:T(1,128)}), f32[32,1,384]{2,1,0:T(1,128)}, u32[]{:S(2)}, u32[]{:S(2)}) %all-to-all-start.5) | async-done | bytes 49184 | tf_op jit(solution)/shard_map/all_to_all | solution.py:511
  76.4 0.8 copy.49
  77.2 0.9 copy-done.8
  78.1 1.0 copy-done.19
  79.1 2.2 %shard_map.131 = (f32[8,3,16,128]{3,2,1,0:T(8,128)S(1)}, f32[8,3,16,128]{3,2,1,0:T(8,128)S(1)}, f32[8,3,16,128]{3,2,1,0:T(8,128)S(1)}, f32[8,3,16,128]{3,2,1,0:T...) custom-call(f32[32,384]{1,0:T(8,128)S(1)} %bitcast.48, f32[8,3,16,128]{3,2,1,0:T(8,128)S(1)} %copy-done.8, ...), custom_call_target="tpu_custom_call" | custom-call | tf_op jit(solution)/shard_map/pallas_call | solution.py:47
  81.4 0.7 copy-done.31
  82.1 0.7 copy-done.33
  82.8 9.0 %all_to_all.125 = f32[32,1,384]{2,1,0:T(1,128)S(1)} all-to-all(f32[32,1,384]{2,1,0:T(1,128)S(1)} %copy.19), channel_id=1, replica_groups=mesh['gx'=4,'gy'=8] {'gx','gy'}, dimensions={0} | all-to-all | bytes 98304 | tf_op jit(solution)/shard_map/all_to_all | solution.py:511
  92.4 0.7 copy.20
  93.1 3.4 %all-to-all-start.7 = ((f32[32,1,384]{2,1,0:T(1,128)}), f32[32,1,384]{2,1,0:T(1,128)}, u32[]{:S(2)}, u32[]{:S(2)}) async-start(f32[32,1,384]{2,1,0:T(1,128)} %copy.20), calls=%async_computation.7 | async-start | bytes 98304 | tf_op jit(solution)/shard_map/all_to_all | solution.py:511
  96.8 6.8 %all-to-all-done.7 = f32[32,1,384]{2,1,0:T(1,128)} async-done(((f32[32,1,384]{2,1,0:T(1,128)}), f32[32,1,384]{2,1,0:T(1,128)}, u32[]{:S(2)}, u32[]{:S(2)}) %all-to-all-start.7) | async-done | bytes 49184 | tf_op jit(solution)/shard_map/all_to_all | solution.py:511
  103.6 0.8 copy.47
  104.4 0.9 copy-done.11
  105.4 1.0 copy-done.21
  106.4 0.9 copy-done.30
  107.3 0.9 copy-done.32
  108.2 0.9 copy-done.34
  109.1 2.3 %shard_map.134 = (f32[8,3,16,128]{3,2,1,0:T(8,128)S(1)}, f32[8,3,16,128]{3,2,1,0:T(8,128)S(1)}, f32[8,3,16,128]{3,2,1,0:T(8,128)S(1)}, f32[8,3,16,128]{3,2,1,0:T...) custom-call(f32[32,384]{1,0:T(8,128)S(1)} %bitcast.56, f32[8,3,16,128]{3,2,1,0:T(8,128)S(1)} %copy-done.11, ...), custom_call_target="tpu_custom_call" | custom-call | tf_op jit(solution)/shard_map/pallas_call | solution.py:47
  111.4 0.7 copy-done.25
  112.1 0.7 copy-done.27
  112.8 9.0 %all_to_all.126 = f32[32,1,384]{2,1,0:T(1,128)S(1)} all-to-all(f32[32,1,384]{2,1,0:T(1,128)S(1)} %copy.21), channel_id=1, replica_groups=mesh['gx'=4,'gy'=8] {'gx','gy'}, dimensions={0} | all-to-all | bytes 98304 | tf_op jit(solution)/shard_map/all_to_all | solution.py:511
  122.4 0.7 copy.22
  123.1 2.6 %all-to-all-start.9 = ((f32[32,1,384]{2,1,0:T(1,128)}), f32[32,1,384]{2,1,0:T(1,128)S(1)}, u32[]{:S(2)}, u32[]{:S(2)}) async-start(f32[32,1,384]{2,1,0:T(1,128)} %copy.22), calls=%async_computation.9 | async-start | bytes 98304 | tf_op jit(solution)/shard_map/all_to_all | solution.py:511
  125.8 7.2 %all-to-all-done.9 = f32[32,1,384]{2,1,0:T(1,128)S(1)} async-done(((f32[32,1,384]{2,1,0:T(1,128)}), f32[32,1,384]{2,1,0:T(1,128)S(1)}, u32[]{:S(2)}, u32[]{:S(2)}) %all-to-all-start.9) | async-done | bytes 49184 | tf_op jit(solution)/shard_map/all_to_all | solution.py:511
  133.0 1.0 copy-done.15
  134.0 0.9 copy-done.24
  134.9 1.9 %shard_map.137 = (f32[8,3,16,128]{3,2,1,0:T(8,128)S(1)}, f32[8,3,16,128]{3,2,1,0:T(8,128)S(1)}, f32[32,128]{1,0:T(8,128)}) custom-call(f32[32,384]{1,0:T(8,128)S(1)} %bitcast.54, f32[8,3,16,128]{3,2,1,0:T(8,128)S(1)} %copy-done.6, f32[24,32,128]{2,1,0:T(8,128)S(1)} %copy-done.15, bf16[8,3,3,16,128]{4,3,2,1,0:T(8,128)(2,1)S(1)} %copy-done.1, ...), custom_call_target="tpu_custom_call" | custom-call | tf_op jit(solution)/shard_map/pallas_call | solution.py:47
  136.9 2.6 %all-to-all-start.10 = ((f32[32,1,128]{2,1,0:T(1,128)}), f32[32,1,128]{2,1,0:T(1,128)S(1)}, u32[]{:S(2)}, u32[]{:S(2)}) async-start(f32[32,1,128]{2,1,0:T(1,128)} %bitcast.13), calls=%async_computation.10 | async-start | bytes 32768 | tf_op jit(solution)/shard_map/all_to_all | solution.py:511
  139.7 6.9 %all-to-all-done.10 = f32[32,1,128]{2,1,0:T(1,128)S(1)} async-done(((f32[32,1,128]{2,1,0:T(1,128)}), f32[32,1,128]{2,1,0:T(1,128)S(1)}, u32[]{:S(2)}, u32[]{:S(2)}) %all-to-all-start.10) | async-done | bytes 16416 | tf_op jit(solution)/shard_map/all_to_all | solution.py:511
  146.7 0.7 copy.54
  147.4 0.7 copy.55
  (88 shorter events, 4.5 us)
Async XLA Ops:
  0.6 3.0 %copy-start.2 = (bf16[8,3,3,16,128]{4,3,2,1,0:T(8,128)(2,1)S(1)}, bf16[8,3,3,16,128]{4,3,2,1,0:T(8,128)(2,1)}, u32[]{:S(2)}) copy-start(bf16[8,3,3,16,128]{4,3,2,1,0:T(8,128)(2,1)} %mobility.9) | copy-start | bytes 884740
  0.6 1.1 copy-start.13
  1.7 0.7 copy-start.35
  2.4 0.7 copy-start.36
  3.2 0.9 copy-start.4
  4.9 16.8 %copy-start.16 = (f32[24,32,128]{2,1,0:T(8,128)}, f32[24,32,128]{2,1,0:T(8,128)S(1)}, u32[]{:S(2)}) copy-start(f32[24,32,128]{2,1,0:T(8,128)S(1)} %get-tuple-element.62.flux_in) | copy-start | bytes 1179652
  5.7 14.6 %all-to-all-start = ((f32[32,1,384]{2,1,0:T(1,128)}), f32[32,1,384]{2,1,0:T(1,128)S(1)}, u32[]{:S(2)}, u32[]{:S(2)}) async-start(f32[32,1,384]{2,1,0:T(1,128)} %copy.13), calls=%async_computation | async-start | bytes 98304 | tf_op jit(solution)/shard_map/all_to_all | solution.py:511
  13.0 7.3 %copy-start.37 = (f32[3,1024]{1,0:T(4,128)S(1)}, f32[3,1024]{1,0:T(4,128)}, u32[]{:S(2)}) copy-start(f32[3,1024]{1,0:T(4,128)} %well_in.1) | copy-start | bytes 36868
  13.0 7.3 %copy-start.38 = (f32[3,1024]{1,0:T(4,128)S(1)}, f32[3,1024]{1,0:T(4,128)}, u32[]{:S(2)}) copy-start(f32[3,1024]{1,0:T(4,128)} %well_out.1) | copy-start | bytes 36868
  20.3 10.9 %copy-start.22 = (f32[8,3,16,128]{3,2,1,0:T(8,128)S(1)}, f32[8,3,16,128]{3,2,1,0:T(8,128)}, u32[]{:S(2)}) copy-start(f32[8,3,16,128]{3,2,1,0:T(8,128)} %right_side.1) | copy-start | bytes 589828
  20.4 10.9 %copy-start = (bf16[4,6,6,16,128]{4,3,2,1,0:T(8,128)(2,1)S(1)}, bf16[4,6,6,16,128]{4,3,2,1,0:T(8,128)(2,1)}, u32[]{:S(2)}) copy-start(bf16[4,6,6,16,128]{4,3,2,1,0:T(8,128)(2,1)} %inverse.7) | copy-start | bytes 1769476
  21.7 9.5 %copy-start.1 = (bf16[8,3,3,16,128]{4,3,2,1,0:T(8,128)(2,1)S(1)}, bf16[8,3,3,16,128]{4,3,2,1,0:T(8,128)(2,1)}, u32[]{:S(2)}) copy-start(bf16[8,3,3,16,128]{4,3,2,1,0:T(8,128)(2,1)} %diag.9) | copy-start | bytes 884740
  21.8 9.4 %copy-start.3 = (bf16[6,8,16,128]{3,2,1,0:T(8,128)(2,1)S(1)}, bf16[6,8,16,128]{3,2,1,0:T(8,128)(2,1)}, u32[]{:S(2)}) copy-start(bf16[6,8,16,128]{3,2,1,0:T(8,128)(2,1)} %face.9) | copy-start | bytes 589828
  31.3 1.0 copy-start.17
  55.5 9.6 %copy-start.7 = (f32[8,3,16,128]{3,2,1,0:T(8,128)}, f32[8,3,16,128]{3,2,1,0:T(8,128)S(1)}, u32[]{:S(2)}) copy-start(f32[8,3,16,128]{3,2,1,0:T(8,128)S(1)} %get-tuple-element.74.vector.applied_hat) | copy-start | bytes 589828
  55.5 9.6 %copy-start.18 = (f32[24,32,128]{2,1,0:T(8,128)}, f32[24,32,128]{2,1,0:T(8,128)S(1)}, u32[]{:S(2)}) copy-start(f32[24,32,128]{2,1,0:T(8,128)S(1)} %get-tuple-element.75.flux_in) | copy-start | bytes 1179652
  65.8 10.6 %all-to-all-start.5 = ((f32[32,1,384]{2,1,0:T(1,128)}), f32[32,1,384]{2,1,0:T(1,128)}, u32[]{:S(2)}, u32[]{:S(2)}) async-start(f32[32,1,384]{2,1,0:T(1,128)} %copy.18), calls=%async_computation.5 | async-start | bytes 98304 | tf_op jit(solution)/shard_map/all_to_all | solution.py:511
  77.2 0.9 copy-start.8
  78.1 1.0 copy-start.19
  81.4 0.7 copy-start.31
  82.1 0.7 copy-start.33
  82.8 9.6 %copy-start.10 = (f32[8,3,16,128]{3,2,1,0:T(8,128)}, f32[8,3,16,128]{3,2,1,0:T(8,128)S(1)}, u32[]{:S(2)}) copy-start(f32[8,3,16,128]{3,2,1,0:T(8,128)S(1)} %get-tuple-element.81.vector.response_hat) | copy-start | bytes 589828
  82.8 9.6 %copy-start.20 = (f32[24,32,128]{2,1,0:T(8,128)}, f32[24,32,128]{2,1,0:T(8,128)S(1)}, u32[]{:S(2)}) copy-start(f32[24,32,128]{2,1,0:T(8,128)S(1)} %get-tuple-element.82.flux_in) | copy-start | bytes 1179652
  82.8 9.6 %copy-start.29 = (f32[8,3,16,128]{3,2,1,0:T(8,128)}, f32[8,3,16,128]{3,2,1,0:T(8,128)S(1)}, u32[]{:S(2)}) copy-start(f32[8,3,16,128]{3,2,1,0:T(8,128)S(1)} %get-tuple-element.88.deeper) | copy-start | bytes 589828
  93.1 10.6 %all-to-all-start.7 = ((f32[32,1,384]{2,1,0:T(1,128)}), f32[32,1,384]{2,1,0:T(1,128)}, u32[]{:S(2)}, u32[]{:S(2)}) async-start(f32[32,1,384]{2,1,0:T(1,128)} %copy.20), calls=%async_computation.7 | async-start | bytes 98304 | tf_op jit(solution)/shard_map/all_to_all | solution.py:511
  104.4 0.9 copy-start.11
  105.4 1.0 copy-start.21
  106.4 0.9 copy-start.30
  107.3 0.9 copy-start.32
  108.2 0.9 copy-start.34
  111.4 0.7 copy-start.25
  112.1 0.7 copy-start.27
  112.8 9.6 %copy-start.5 = (f32[8,3,16,128]{3,2,1,0:T(8,128)}, f32[8,3,16,128]{3,2,1,0:T(8,128)S(1)}, u32[]{:S(2)}) copy-start(f32[8,3,16,128]{3,2,1,0:T(8,128)S(1)} %get-tuple-element.91.vector.applied_hat) | copy-start | bytes 589828
  112.8 9.6 %copy-start.14 = (f32[24,32,128]{2,1,0:T(8,128)}, f32[24,32,128]{2,1,0:T(8,128)S(1)}, u32[]{:S(2)}) copy-start(f32[24,32,128]{2,1,0:T(8,128)S(1)} %get-tuple-element.92.flux_in) | copy-start | bytes 1179652
  112.8 9.6 %copy-start.23 = (f32[8,3,16,128]{3,2,1,0:T(8,128)}, f32[8,3,16,128]{3,2,1,0:T(8,128)S(1)}, u32[]{:S(2)}) copy-start(f32[8,3,16,128]{3,2,1,0:T(8,128)S(1)} %get-tuple-element.95.residual) | copy-start | bytes 589828
  121.8 11.2 %copy-start.26 = (f32[8,3,16,128]{3,2,1,0:T(8,128)S(1)}, f32[8,3,16,128]{3,2,1,0:T(8,128)}, u32[]{:S(2)}) copy-start(f32[8,3,16,128]{3,2,1,0:T(8,128)} %copy-done.25) | copy-start | bytes 589828
  121.8 11.2 %copy-start.28 = (f32[8,3,16,128]{3,2,1,0:T(8,128)S(1)}, f32[8,3,16,128]{3,2,1,0:T(8,128)}, u32[]{:S(2)}) copy-start(f32[8,3,16,128]{3,2,1,0:T(8,128)} %copy-done.27) | copy-start | bytes 589828
  122.4 10.6 %copy-start.6 = (f32[8,3,16,128]{3,2,1,0:T(8,128)S(1)}, f32[8,3,16,128]{3,2,1,0:T(8,128)}, u32[]{:S(2)}) copy-start(f32[8,3,16,128]{3,2,1,0:T(8,128)} %copy-done.5) | copy-start | bytes 589828
  123.1 9.9 %all-to-all-start.9 = ((f32[32,1,384]{2,1,0:T(1,128)}), f32[32,1,384]{2,1,0:T(1,128)S(1)}, u32[]{:S(2)}, u32[]{:S(2)}) async-start(f32[32,1,384]{2,1,0:T(1,128)} %copy.22), calls=%async_computation.9 | async-start | bytes 98304 | tf_op jit(solution)/shard_map/all_to_all | solution.py:511
  133.0 1.0 copy-start.15
  134.0 0.9 copy-start.24
  134.9 4.5 %copy-start.9 = (f32[8,3,16,128]{3,2,1,0:T(8,128)S(1)}, f32[8,3,16,128]{3,2,1,0:T(8,128)}, u32[]{:S(2)}) copy-start(f32[8,3,16,128]{3,2,1,0:T(8,128)} %copy-done.7) | copy-start | bytes 589828
  134.9 4.5 %copy-start.12 = (f32[8,3,16,128]{3,2,1,0:T(8,128)S(1)}, f32[8,3,16,128]{3,2,1,0:T(8,128)}, u32[]{:S(2)}) copy-start(f32[8,3,16,128]{3,2,1,0:T(8,128)} %copy-done.10) | copy-start | bytes 589828
  136.9 9.7 %all-to-all-start.10 = ((f32[32,1,128]{2,1,0:T(1,128)}), f32[32,1,128]{2,1,0:T(1,128)S(1)}, u32[]{:S(2)}, u32[]{:S(2)}) async-start(f32[32,1,128]{2,1,0:T(1,128)} %bitcast.13), calls=%async_computation.10 | async-start | bytes 32768 | tf_op jit(solution)/shard_map/all_to_all | solution.py:511

commit v2 on v1

v2 whole, which is shorter than its diff:
```python
import functools

import jax
import jax.numpy as jnp
from jax import lax
from jax.experimental import pallas as pl
from jax.experimental.pallas import tpu as pltpu
from jax.sharding import PartitionSpec as P

ITERS = 2
AXES = ("gx", "gy")
LANES = 128
SUBS = 8
F32 = jnp.float32
BF16 = jnp.bfloat16
SCOPED = 16 * 1024 * 1024


class Geometry:
    def __init__(self, vector_shape, table_shape, inverse_shape, n_gy):
        self.layers, self.comps, self.rows, self.cols = vector_shape
        self.devices, self.cap = table_shape
        self.wells, self.segs = inverse_shape[:2]
        self.n_gy = n_gy
        self.tile_rows = self.layers * self.rows
        self.half_rows = self.tile_rows // 2
        self.faces = self.layers * self.comps
        self.per = LANES // self.cap
        self.groups = -(-self.devices // self.per)
        self.groups_pad = -(-self.groups // SUBS) * SUBS
        self.slots = self.groups * LANES
        self.vector = (self.layers, self.comps, self.rows, self.cols)
        self.flux = (self.faces * self.rows + 2 * SUBS, self.cols)
        self.tile = (self.rows, LANES)
        assert self.cols == LANES and self.segs == LANES and self.rows == 2 * SUBS
        assert self.faces + SUBS <= self.devices and 2 * self.faces <= LANES
        assert 3 * self.cap <= LANES

    def pieces(self):
        for k in range(self.per):
            low = k * self.groups
            count = min(self.groups, self.devices - low)
            if count > 0:
                yield k, low, count

    def tiles(self):
        for z in range(self.layers):
            for c in range(self.comps):
                yield z, c

    def base(self, j):
        return SUBS + j * self.rows


HELD = pl.BlockSpec(memory_space=pltpu.VMEM)
FAR = pl.BlockSpec(memory_space=pltpu.HBM)


def call(body, outs, args, far=(), scratch=(), out_far=False):
    held = [pltpu.with_memory_space_constraint(a, pltpu.VMEM) for a in args]
    far = [pltpu.with_memory_space_constraint(a, pltpu.HBM) for a in far]
    shapes = [jax.ShapeDtypeStruct(*o) if out_far else pltpu.VMEM(*o) for o in outs]
    return pl.pallas_call(
        body,
        out_shape=tuple(shapes),
        in_specs=[HELD] * len(held) + [FAR] * len(far),
        out_specs=(FAR if out_far else HELD,) * len(outs),
        scratch_shapes=list(scratch),
        compiler_params=pltpu.CompilerParams(vmem_limit_bytes=SCOPED),
    )(*held, *far)


def iota(shape, dim):
    return lax.broadcasted_iota(jnp.int32, shape, dim)


def take_lanes(table, index):
    return jnp.take_along_axis(table, index, axis=1, mode="promise_in_bounds")


def spread(row, shape):
    return jnp.broadcast_to(row, shape)


def total(block):
    return jnp.sum(jnp.sum(block, axis=0, keepdims=True), axis=1, keepdims=True)


def one_hot(index, size):
    rows = spread(index, (size, LANES))
    return jnp.where(rows == iota(rows.shape, 0), 1.0, 0.0).astype(BF16)


def pack_slots(geo, block_ref, lane, packed_ref):
    packed_ref[...] = jnp.zeros_like(packed_ref)
    start = lane // LANES * LANES
    for k, low, count in geo.pieces():
        part = block_ref[low : low + count, start : start + LANES]
        shift = (k * geo.cap - lane) % LANES
        part = pltpu.roll(part, shift, 1) if shift else part
        at = iota(part.shape, 1)
        mine = (at >= k * geo.cap) & (at < (k + 1) * geo.cap)
        packed_ref[0:count, :] = jnp.where(mine, part, packed_ref[0:count, :])


def unpack_slots(geo, packed, lane, block_ref):
    for k, low, count in geo.pieces():
        shift = (lane - k * geo.cap) % LANES
        part = pltpu.roll(packed, shift, 1) if shift else packed
        part = part[0:count]
        at = iota(part.shape, 1)
        mine = (at >= lane) & (at < lane + geo.cap)
        block_ref[low : low + count, 0:LANES] = jnp.where(
            mine, part, block_ref[low : low + count, 0:LANES]
        )


def write_faces(geo, flux, send):
    one, two, three = LANES, 2 * LANES, 3 * LANES
    if geo.devices > geo.faces + SUBS:
        send[geo.faces + SUBS :, one:three] = jnp.zeros((geo.devices - geo.faces - SUBS, 2 * LANES), F32)
    send[0 : geo.faces, one:two] = flux[pl.ds(geo.base(0), geo.faces, stride=geo.rows), :]
    send[0 : geo.faces, two:three] = flux[pl.ds(geo.base(0) + geo.rows - 1, geo.faces, stride=geo.rows), :]
    at = iota(geo.tile, 1) >> 1
    edges = jnp.zeros(geo.tile, F32)
    for j in range(geo.faces):
        turned = pltpu.roll(flux[geo.base(j) : geo.base(j) + geo.rows, :], 2 * j + 1, 1)
        edges = jnp.where(at == j, turned, edges)
    send[geo.faces : geo.faces + SUBS, one:two] = edges[:SUBS]
    send[geo.faces : geo.faces + SUBS, two:three] = edges[SUBS:]


def write_flux(geo, mobility, vector, flux):
    flux[0:SUBS, :] = jnp.zeros((SUBS, LANES), F32)
    flux[geo.base(geo.faces) :, :] = jnp.zeros((SUBS, LANES), F32)
    for z in range(geo.layers):
        v = [vector[z, b] for b in range(3)]
        for a in range(3):
            block = mobility[z, a, 0].astype(F32) * v[0]
            block += mobility[z, a, 1].astype(F32) * v[1]
            block += mobility[z, a, 2].astype(F32) * v[2]
            base = geo.base(3 * z + a)
            flux[base : base + geo.rows, :] = block


def gather_cells(geo, vector, rowp, lanep, finish):
    shape = (SUBS, LANES)
    for g in range(geo.groups):
        lane = spread(lanep[g : g + 1, :], shape)
        row = spread(rowp[g : g + 1, :], shape) - iota(shape, 0)
        kept = [jnp.zeros(shape, F32) for _ in range(3)]
        for z in range(geo.layers):
            for h in range(geo.rows // SUBS):
                mine = row == z * geo.rows + h * SUBS
                for c in range(3):
                    found = take_lanes(vector[z, c, h * SUBS : (h + 1) * SUBS, :], lane)
                    kept[c] = jnp.where(mine, found, kept[c])
        finish(g, kept)


def precondition(geo, inverse, source, target):
    for h in range(geo.layers // 2):
        v = [source(2 * h + f // 3, f % 3) for f in range(6)]
        for e in range(6):
            block = inverse[h, e, 0].astype(F32) * v[0]
            for f in range(1, 6):
                block += inverse[h, e, f].astype(F32) * v[f]
            target(2 * h + e // 3, e % 3, block)


def first_body(geo, *refs):
    far, refs = refs[:7], refs[7:]
    (flux, send, rowp, lanep, spot_hot, hi, lo, inv_dev, inv_pos, turned, guess, mobility, well_in, well_out), refs = refs[:14], refs[14:]
    cells, slots, inverse, wide, ints, packed, sems = refs
    targets = (cells, slots, guess, mobility, inverse, well_in, well_out)
    copies = [pltpu.make_async_copy(source, target, sems.at[i]) for i, (source, target) in enumerate(zip(far, targets))]
    for copy in copies:
        copy.start()
    wide[...] = jnp.zeros_like(wide)
    copies[0].wait()
    wide[:, 0 : geo.cap] = cells[...] + 1
    pack_slots(geo, wide, 0, ints)
    index = ints[...] - 1
    rowp[...] = index >> 7
    lanep[...] = index & (LANES - 1)
    copies[1].wait()
    slot_tables(geo, slots, hi, lo, inv_dev, inv_pos, wide, ints)
    copies[2].wait()
    copies[3].wait()
    write_flux(geo, mobility, guess, flux)
    write_faces(geo, flux, send)
    send[:, 0:LANES] = jnp.zeros((geo.devices, LANES), F32)
    packed[...] = jnp.zeros_like(packed)

    def finish(g, kept):
        for c in range(3):
            packed[c, g : g + 1, :] = jnp.sum(kept[c], axis=0, keepdims=True)

    gather_cells(geo, guess, rowp, lanep, finish)
    for c in range(3):
        unpack_slots(geo, packed[c], c * geo.cap, send)
    for g in range(geo.groups):
        row, lane = rowp[g : g + 1, :], lanep[g : g + 1, :]
        upper = jnp.where(row >= geo.half_rows, LANES, 0)
        spot_hot[:, g * LANES : (g + 1) * LANES] = one_hot(upper + lane, 2 * LANES)
    copies[4].wait()
    for w in range(geo.wells):
        turned[w] = inverse[w].T
    copies[5].wait()
    copies[6].wait()


def slot_tables(geo, slot_ref, hi, lo, inv_dev, inv_pos, wide, packed):
    wide[:, 0 : geo.cap] = slot_ref[...] + 1
    slots = wide[...] - 1
    hi[...] = slots >> 7
    lo[...] = slots & (LANES - 1)
    pack_slots(geo, wide, 0, packed)
    slots = packed[...] - 1
    slot_hi = slots >> 7
    slot_lo = slots & (LANES - 1)
    at = iota((geo.wells, LANES), 1)
    piece = lax.div(at, geo.cap)
    position = (lax.rem(at, geo.cap) + 1).astype(F32)
    found = jnp.zeros((2 * geo.wells, LANES), F32)
    for g in range(geo.groups):
        well = spread(slot_hi[g : g + 1], (geo.wells, LANES)) == iota((geo.wells, LANES), 0)
        device = (piece * geo.groups + (g + 1)).astype(F32)
        marks = jnp.concatenate([jnp.where(well, device, 0.0), jnp.where(well, position, 0.0)], axis=0)
        hot = one_hot(slot_lo[g : g + 1], LANES)
        found += lax.dot_general(marks.astype(BF16), hot, (((1,), (1,)), ((), ())), preferred_element_type=F32)
    inv_dev[...] = found[: geo.wells].astype(jnp.int32) - 1
    inv_pos[...] = jnp.maximum(found[geo.wells :].astype(jnp.int32) - 1, 0)


def relay(geo, came, back):
    shape = (geo.devices, LANES)
    at = iota(shape, 0)
    even = (iota(shape, 1) & 1) == 0
    within = lax.rem(at, geo.n_gy)
    faces = jnp.full(shape, lax.axis_index(AXES), jnp.int32) < geo.faces
    up, down, count = geo.n_gy, geo.devices - geo.n_gy, geo.devices
    one = came[:, LANES : 2 * LANES]
    two = came[:, 2 * LANES : 3 * LANES]
    after = jnp.where(at < down, pltpu.roll(one, down, 0), 0.0)
    before = jnp.where(at >= up, pltpu.roll(two, up, 0), 0.0)

    def beside(block):
        low = jnp.where(within > 0, pltpu.roll(pltpu.roll(block, 1, 1), 1, 0), 0.0)
        high = jnp.where(within < geo.n_gy - 1, pltpu.roll(pltpu.roll(block, LANES - 1, 1), count - 1, 0), 0.0)
        return jnp.where(even, high, low)

    back[:, LANES : 2 * LANES] = jnp.where(faces, after, beside(one))
    back[:, 2 * LANES : 3 * LANES] = jnp.where(faces, before, beside(two))


def at_segments(geo, came, inv_dev, inv_pos, offset):
    shape = (geo.wells, LANES)
    device = inv_dev[...]
    position = inv_pos[...] + offset
    kept = jnp.zeros(shape, F32)
    for s in range(geo.devices):
        found = take_lanes(spread(came[s : s + 1, 0:LANES], shape), position)
        kept = jnp.where(device == s, found, kept)
    return kept


def at_slots(geo, rows, hi, lo):
    shape = (geo.devices, LANES)
    kept = jnp.zeros(shape, F32)
    for w in range(geo.wells):
        found = take_lanes(spread(rows[w], shape), lo)
        kept = jnp.where(hi == w, found, kept)
    return kept


def solve_segments(geo, rate, turned):
    rate_t = rate.T
    rows = []
    for w in range(geo.wells):
        rows.append(jnp.sum(turned[w] * rate_t[:, w : w + 1], axis=0, keepdims=True))
    return rows


def owner_first_body(geo, came, inv_dev, inv_pos, hi_ref, lo_ref, turned, well_in, well_out, back):
    hi, lo = hi_ref[...], lo_ref[...]
    rows_in = [[well_in[c : c + 1, w * LANES : (w + 1) * LANES] for w in range(geo.wells)] for c in range(3)]
    rows_out = [[well_out[c : c + 1, w * LANES : (w + 1) * LANES] for w in range(geo.wells)] for c in range(3)]
    rate = jnp.zeros((geo.wells, LANES), F32)
    for c in range(3):
        rate += jnp.concatenate(rows_in[c], axis=0) * at_segments(geo, came, inv_dev, inv_pos, c * geo.cap)
    back[:, 0:LANES] = at_slots(geo, solve_segments(geo, rate, turned), hi, lo)
    relay(geo, came, back)
    for place, rows in ((3, rows_in), (4, rows_out)):
        block = jnp.zeros((geo.devices, LANES), F32)
        for c in range(3):
            part = at_slots(geo, rows[c], hi, lo)
            block += pltpu.roll(part, c * geo.cap, 1) if c else part
        back[:, place * LANES : (place + 1) * LANES] = block


def owner_body(geo, came, inv_dev, inv_pos, hi_ref, lo_ref, turned, back, sums):
    rate = at_segments(geo, came, inv_dev, inv_pos, 0)
    back[:, 0:LANES] = at_slots(geo, solve_segments(geo, rate, turned), hi_ref[...], lo_ref[...])
    relay(geo, came, back)
    sums[...] = spread(jnp.sum(came[:, 0:LANES], axis=0, keepdims=True), sums.shape)


def scatter_terms(geo, came, coeff_out, rowp, spot_hot, packed, left, spots):
    pack_slots(geo, came, 0, packed)
    rate = packed[...]
    parts = []
    for c in range(3):
        value = coeff_out[c] * rate
        high = value.astype(BF16)
        parts += [high, (value - high.astype(F32)).astype(BF16)]
    n = geo.half_rows
    row = rowp[...]
    row = jnp.where(row >= n, row - n, row)
    for g in range(geo.groups):
        hot = one_hot(row[g : g + 1], n)
        for i, part in enumerate(parts):
            left[i * n : (i + 1) * n, g * LANES : (g + 1) * LANES] = hot * spread(part[g : g + 1], hot.shape)
    result = lax.dot_general(left[...], spot_hot[...], (((1,), (1,)), ((), ())), preferred_element_type=F32)
    for c in range(3):
        i = 2 * c * n
        summed = result[i : i + n] + result[i + n : i + 2 * n]
        for h in range(2):
            low = c * geo.tile_rows + h * n
            spots[low : low + n, :] = summed[:, h * LANES : (h + 1) * LANES]


def apply_operator(geo, came, vector, flux, diag, face, spots, store):
    at_row, at_lane = iota((SUBS, LANES), 0), iota(geo.tile, 1)
    one, two, three = LANES, 2 * LANES, 3 * LANES
    last = geo.faces + SUBS
    edges = jnp.concatenate([came[geo.faces : last, one:two], came[geo.faces : last, two:three]], axis=0)
    for z in range(geo.layers):
        f = [face[n, z].astype(F32) for n in range(6)]
        v = [vector[z, b] for b in range(3)]
        for a in range(3):
            j = 3 * z + a
            base = geo.base(j)
            block = flux[base : base + geo.rows, :]
            first = jnp.where(at_row == 0, spread(came[j : j + 1, two:three], at_row.shape), flux[base - 1 : base - 1 + SUBS, :])
            under = jnp.concatenate([first, flux[base - 1 + SUBS : base - 1 + geo.rows, :]], axis=0)
            final = jnp.where(at_row == SUBS - 1, spread(came[j : j + 1, one:two], at_row.shape), flux[base + 1 + SUBS : base + 1 + geo.rows, :])
            over = jnp.concatenate([flux[base + 1 : base + 1 + SUBS, :], final], axis=0)
            ends = pltpu.roll(edges, LANES - 1 - 2 * j, 1)
            left = jnp.where(at_lane == 0, ends, pltpu.roll(block, 1, 1))
            right = jnp.where(at_lane == LANES - 1, ends, pltpu.roll(block, LANES - 1, 1))
            beside = f[0] * under + f[1] * over + f[2] * left + f[3] * right
            if z > 0:
                beside += f[4] * flux[base - 3 * geo.rows : base - 2 * geo.rows, :]
            if z + 1 < geo.layers:
                beside += f[5] * flux[base + 3 * geo.rows : base + 4 * geo.rows, :]
            own = diag[z, a, 0].astype(F32) * v[0]
            own += diag[z, a, 1].astype(F32) * v[1]
            own += diag[z, a, 2].astype(F32) * v[2]
            low = a * geo.tile_rows + z * geo.rows
            store(z, a, own - beside - spots[low : low + geo.rows, :])


def send_next(geo, source, inverse, mobility, rowp, lanep, coeff_in, dots, ahead, flux, send, packed):
    def put(z, c, block):
        ahead[z, c] = block

    precondition(geo, inverse, lambda z, c: source[z, c], put)
    write_flux(geo, mobility, ahead, flux)
    write_faces(geo, flux, send)
    at = iota((1, LANES), 1)
    row = jnp.zeros((1, LANES), F32)
    for n, dot in enumerate(dots):
        row = jnp.where(at == geo.cap + n, spread(total(dot), (1, LANES)), row)
    send[:, 0:LANES] = spread(row, (geo.devices, LANES))
    packed[...] = jnp.zeros_like(packed)

    def finish(g, kept):
        rate = kept[0] * spread(coeff_in[0, g : g + 1, :], kept[0].shape)
        rate += kept[1] * spread(coeff_in[1, g : g + 1, :], kept[0].shape)
        rate += kept[2] * spread(coeff_in[2, g : g + 1, :], kept[0].shape)
        packed[g : g + 1, :] = jnp.sum(rate, axis=0, keepdims=True)

    gather_cells(geo, ahead, rowp, lanep, finish)
    unpack_slots(geo, packed[...], 0, send)


def stage_body(geo, rule, n_in, n_out, goes_on, *refs):
    refs = list(refs)

    def take(n):
        got, refs[:n] = refs[:n], []
        return got

    came, vector, flux_in, rowp, lanep, spot_hot = take(6)
    inputs = take(n_in)
    diag, face, *hats = take(4 if goes_on else 2)
    outputs = take(n_out)
    following = take(3) if goes_on else take(1)
    packed, left, spots = take(3)
    coeff_in, coeff_out, store, source, dots = rule(came, packed, inputs, outputs)
    scatter_terms(geo, came, coeff_out, rowp, spot_hot, packed, left, spots)
    apply_operator(geo, came, vector, flux_in, diag, face, spots, store)
    if goes_on:
        ahead, flux, send = following
        send_next(geo, source, *hats, rowp, lanep, coeff_in, dots, ahead, flux, send, packed)
    else:
        at = iota((1, LANES), 1)
        row = jnp.where(at == 0, spread(total(dots[0]), (1, LANES)), spread(total(dots[1]), (1, LANES)))
        following[0][...] = spread(row, following[0].shape)


def zeros(geo, count):
    return [jnp.zeros(geo.tile, F32) for _ in range(count)]


def pick(sums, geo, n):
    return sums[0:1, geo.cap + n : geo.cap + n + 1]


def keep(ref, value):
    ref[...] = spread(value, ref.shape)


def residual_rule(geo, came, packed, inputs, outputs):
    (right_side,) = inputs
    shadow, coeff_in, coeff_out = outputs
    for c in range(3):
        pack_slots(geo, came, 3 * LANES + c * geo.cap, packed)
        coeff_in[c] = packed[...]
        pack_slots(geo, came, 4 * LANES + c * geo.cap, packed)
        coeff_out[c] = packed[...]
    dots = zeros(geo, 1)

    def store(z, c, image):
        value = right_side[z, c] - image
        shadow[z, c] = value
        dots[0] += value * value

    return coeff_in, coeff_out, store, shadow, dots


def image_rule(geo, came, packed, inputs, outputs):
    coeff_in, coeff_out, shadow = inputs
    (applied,) = outputs
    dots = zeros(geo, 1)

    def store(z, c, image):
        applied[z, c] = image
        dots[0] += shadow[z, c] * image

    return coeff_in, coeff_out, store, applied, dots


def half_rule(geo, came, packed, inputs, outputs):
    coeff_in, coeff_out, shadow, rho_sums, rho_at, sums, residual, applied, behind = inputs
    step_out, deeper, half, response = outputs
    step = rho_sums[0:1, rho_at : rho_at + 1] / pick(sums, geo, 0)
    keep(step_out, step)
    step = spread(step, geo.tile)
    dots = zeros(geo, 4)

    def store(z, c, image):
        deeper[z, c] = image
        s = residual[z, c] - step * applied[z, c]
        t = behind[z, c] - step * image
        half[z, c] = s
        response[z, c] = t
        dots[0] += t * s
        dots[1] += t * t
        dots[2] += shadow[z, c] * t
        dots[3] += shadow[z, c] * s

    return coeff_in, coeff_out, store, response, dots


def next_rule(geo, came, packed, inputs, outputs):
    coeff_in, coeff_out, shadow, rho_sums, rho_at, step_in, sums, half, response, applied, deeper, search, moved = inputs
    rho_out, residual_next, behind_next, applied_next, search_next, moved_next = outputs
    smoothing = pick(sums, geo, 0) / pick(sums, geo, 1)
    rho_next = pick(sums, geo, 3) - smoothing * pick(sums, geo, 2)
    step = step_in[0:1, 0:1]
    momentum = (rho_next / rho_sums[0:1, rho_at : rho_at + 1]) * (step / smoothing)
    keep(rho_out, rho_next)
    smoothing, momentum, step = (spread(x, geo.tile) for x in (smoothing, momentum, step))
    dots = zeros(geo, 1)

    def store(z, c, image):
        t = response[z, c]
        s = half[z, c]
        p = search[z, c]
        v = applied[z, c]
        r = s - smoothing * t
        w = t - smoothing * image
        v_next = w + momentum * (v - smoothing * deeper[z, c])
        residual_next[z, c] = r
        behind_next[z, c] = w
        applied_next[z, c] = v_next
        search_next[z, c] = r + momentum * (p - smoothing * v)
        by = step * p + smoothing * s
        moved_next[z, c] = by if moved is None else moved[z, c] + by
        dots[0] += shadow[z, c] * v_next

    return coeff_in, coeff_out, store, applied_next, dots


def last_rule(geo, came, packed, inputs, outputs):
    coeff_out, rho_sums, rho_at, sums, residual, applied, behind, search, moved = inputs
    half, response, moved_next = outputs
    step = spread(rho_sums[0:1, rho_at : rho_at + 1] / pick(sums, geo, 0), geo.tile)
    dots = zeros(geo, 2)

    def store(z, c, image):
        s = residual[z, c] - step * applied[z, c]
        t = behind[z, c] - step * image
        half[z, c] = s
        response[z, c] = t
        by = step * search[z, c]
        moved_next[z, c] = by if moved is None else moved[z, c] + by
        dots[0] += t * s
        dots[1] += t * t

    return None, coeff_out, store, None, dots


def finish_body(geo, came, moved, half, response, guess, inverse, solution_out, residual_out, solution, residual, sems):
    sums = jnp.sum(came[...], axis=0, keepdims=True)
    smoothing = spread(sums[:, 0:1] / sums[:, 1:2], geo.tile)
    copies = []

    def leave(source, target, layer, sem):
        copies.append(pltpu.make_async_copy(source.at[layer], target.at[layer], sem))
        copies[-1].start()

    for z, c in geo.tiles():
        residual[z, c] = half[z, c] - smoothing * response[z, c]
        if c + 1 == geo.comps:
            leave(residual, residual_out, z, sems.at[0, z])

    def put(z, c, block):
        solution[z, c] = guess[z, c] + block
        if z % 2 and c + 1 == geo.comps:
            leave(solution, solution_out, z - 1, sems.at[1, z - 1])
            leave(solution, solution_out, z, sems.at[1, z])

    precondition(geo, inverse, lambda z, c: moved[z, c] + smoothing * half[z, c], put)
    for copy in copies:
        copy.wait()


def exchange(rows):
    return lax.all_to_all(rows, AXES, split_axis=0, concat_axis=0, tiled=True)


def per_device(right_side, guess, diag, mobility, face, inverse, perf_cell, perf_slot, well_in, well_out, well_inverse):
    geo = Geometry(right_side.shape, perf_cell.shape[1:], well_inverse.shape, lax.axis_size("gy"))
    ints = jnp.int32
    block = (geo.devices, LANES)
    packed = (geo.groups_pad, LANES)
    seg = (geo.wells, LANES)
    wide = ((geo.devices, 3 * LANES), F32)
    small = ((SUBS, LANES), F32)
    vec = (geo.vector, F32)
    coeffs = ((3,) + packed, F32)
    sent = [vec, (geo.flux, F32), wide]

    table = (perf_cell.shape[1:], ints)
    flux, send, rowp, lanep, spot_hot, hi, lo, inv_dev, inv_pos, turned, guess_held, mobility, well_in, well_out = call(
        functools.partial(first_body, geo),
        [(geo.flux, F32), wide, (packed, ints), (packed, ints), ((2 * LANES, geo.slots), BF16), (block, ints), (block, ints),
         (seg, ints), (seg, ints), (well_inverse.shape, F32), vec, (mobility.shape, BF16), (well_in.shape, F32), (well_out.shape, F32)],
        [], far=[perf_cell[0], perf_slot[0], guess, mobility, well_inverse, well_in, well_out],
        scratch=[pltpu.VMEM(*table), pltpu.VMEM(*table), pltpu.VMEM(well_inverse.shape, F32), pltpu.VMEM(block, ints),
                 pltpu.VMEM(packed, ints), pltpu.VMEM((3,) + packed, F32), pltpu.SemaphoreType.DMA((7,))],
    )
    owner_tables = [inv_dev, inv_pos, hi, lo, turned]
    scratch = [pltpu.VMEM(packed, F32), pltpu.VMEM((6 * geo.half_rows, geo.slots), BF16), pltpu.VMEM((3 * geo.tile_rows, LANES), F32)]

    def stage(rule, outs, came, vector, flux, inputs, goes_on=True):
        arrays = [i for i in inputs if i is not None and not isinstance(i, int)]

        def placed(came, packed, refs, out_refs):
            rest = list(refs)
            return rule(geo, came, packed, [i if i is None or isinstance(i, int) else rest.pop(0) for i in inputs], out_refs)

        return call(
            functools.partial(stage_body, geo, placed, len(arrays), len(outs), goes_on),
            outs + (sent if goes_on else [(block, F32)]),
            [came, vector, flux, rowp, lanep, spot_hot] + arrays + [diag, face] + ([inverse, mobility] if goes_on else []), scratch=scratch,
        )

    def owner(send):
        back, sums = call(functools.partial(owner_body, geo), [wide, small], [exchange(send)] + owner_tables)
        return exchange(back), sums

    (back,) = call(
        functools.partial(owner_first_body, geo), [((geo.devices, 5 * LANES), F32)], [exchange(send)] + owner_tables + [well_in, well_out]
    )
    shadow, coeff_in, coeff_out, ahead, flux, send = stage(residual_rule, [vec, coeffs, coeffs], exchange(back), guess_held, flux, [right_side])
    always = [coeff_in, coeff_out, shadow]
    came, sums = owner(send)
    rho, rho_at = sums, geo.cap
    applied, ahead, flux, send = stage(image_rule, [vec], came, ahead, flux, always)
    residual, search, behind, moved = shadow, shadow, applied, None
    for iteration in range(ITERS):
        came, sums = owner(send)
        if iteration + 1 == ITERS:
            half, response, moved, send = stage(
                last_rule, [vec] * 3, came, ahead, flux,
                [coeff_out, rho, rho_at, sums, residual, applied, behind, search, moved], goes_on=False,
            )
            break
        step, deeper, half, response, ahead, flux, send = stage(
            half_rule, [small] + [vec] * 3, came, ahead, flux, always + [rho, rho_at, sums, residual, applied, behind]
        )
        came, sums = owner(send)
        rho, residual, behind, applied, search, moved, ahead, flux, send = stage(
            next_rule, [small] + [vec] * 5, came, ahead, flux,
            always + [rho, rho_at, step, sums, half, response, applied, deeper, search, moved],
        )
        rho_at = 0
    return call(
        functools.partial(finish_body, geo), [vec] * 2, [exchange(send), moved, half, response, guess, inverse],
        scratch=[pltpu.VMEM(*vec), pltpu.VMEM(*vec), pltpu.SemaphoreType.DMA((2, geo.layers))], out_far=True,
    )


def solution(mesh):
    in_specs = (
        P(None, None, "gx", "gy"),
        P(None, None, "gx", "gy"),
        P(None, None, None, "gx", "gy"),
        P(None, None, None, "gx", "gy"),
        P(None, None, "gx", "gy"),
        P(None, None, None, "gx", "gy"),
        P(AXES, None, None),
        P(AXES, None, None),
        P(None, AXES),
        P(None, AXES),
        P(AXES, None, None),
    )
    out_specs = (P(None, None, "gx", "gy"), P(None, None, "gx", "gy"))
    return jax.shard_map(per_device, mesh=mesh, in_specs=in_specs, out_specs=out_specs, check_vma=False)
```

time: 149 us -> 121 us (0.81)
  blocking collectives: 54.4 us -> 105 us
  waiting for transfers between devices: 35.3 us -> 0 us
  local copies, waits for them, and re-layouts: 21.4 us -> 0.62 us
  starting transfers between devices: 19.1 us -> 0 us
  Pallas kernels: 16.8 us -> 14.6 us
    all_to_all x6 -> x11, blocking collectives: 54.4 us -> 105 us  [exchange(): return lax.all_to_all(rows, AXES, split_axis=0, concat_axis=0, tiled=True)]
    all_to_all x5 -> x0, waiting for transfers between devices: 35.3 us -> none  [exchange(): return lax.all_to_all(rows, AXES, split_axis=0, concat_axis=0, tiled=True)]
    all_to_all x5 -> x0, starting transfers between devices: 19.1 us -> none  [exchange(): return lax.all_to_all(rows, AXES, split_axis=0, concat_axis=0, tiled=True)]
    unnamed x90 -> x20, local copies, waits for them, and re-layouts: 18.3 us -> 0.07 us
    all_to_all x10, local copies, waits for them, and re-layouts: 3.12 us -> 0.56 us  [exchange(): return lax.all_to_all(rows, AXES, split_axis=0, concat_axis=0, tiled=True)]
    pallas_call x19 -> x12, Pallas kernels: 16.8 us -> 14.6 us  [call(): pl.pallas_call(body, out_shape=tuple(shapes), in_specs=[HELD] * len(held)...]
  transfers between devices with their start and end apart: 5 -> 0, of which waited for: 5 -> 0; matrix products, arithmetic and copies ran while one was open for 0% -> 0% of each run, Pallas kernels for 1% -> 0%
where the time goes in v2:
time: 121 us
  blocking collectives  105 us (87%)
  Pallas kernels  14.6 us (12%)
    all_to_all x11, blocking collectives, exchange(): return lax.all_to_all(rows, AXES, split_axis=0, concat_axis=0, tiled=True)  105 us
    pallas_call x12, Pallas kernels, call(): pl.pallas_call(body, out_shape=tuple(shapes), in_specs=[HELD] * len(held)...  14.6 us

profile of v2, /device:TPU:0, one launch (start us, length us, event | category | flops | bytes accessed | tf_op | source)
XLA Modules:
  0.0 120.8 jit_solution(5766201269659016103)
XLA Ops:
  0.6 2.6 %shard_map.122 = (f32[400,128]{1,0:T(8,128)S(1)}, f32[32,384]{1,0:T(8,128)S(1)}, s32[16,128]{1,0:T(8,128)S(1)}, s32[16,128]{1,0:T(8,128)S(1)}, bf16[256,1408]{1,...) custom-call(s32[32,40]{1,0:T(8,128)} %bitcast.68, ...), custom_call_target="tpu_custom_call" | custom-call | tf_op jit(solution)/shard_map/pallas_call | solution.py:63
  3.2 0.1 copy.13
  3.3 14.4 %all_to_all.121 = f32[32,1,384]{2,1,0:T(1,128)S(1)} all-to-all(f32[32,1,384]{2,1,0:T(1,128)S(1)} %copy.13), channel_id=1, replica_groups=mesh['gx'=4,'gy'=8] {'gx','gy'}, dimensions={0} | all-to-all | bytes 98304 | tf_op jit(solution)/shard_map/all_to_all | solution.py:552
  17.7 0.0 copy-start.4
  17.7 0.0 copy-start
  17.7 1.4 %shard_map.123 = f32[32,640]{1,0:T(8,128)S(1)} custom-call(f32[32,384]{1,0:T(8,128)S(1)} %bitcast.50, s32[8,128]{1,0:T(8,128)S(1)} %get-tuple-element.55.inv_dev, s32[8,128]{1,0:T(8,128)S(1)} %get-tuple-element.56.inv_pos, s32[32,128]{1,0:T(8,128)S(1)} %get-tuple-element.57.hi_ref, s32[32,128]{1,0:T(8,128)S(1)} %get-tuple-element.58.lo_ref, ...), custom_call_target="tpu_custom_call" | custom-call | tf_op jit(solution)/shard_map/pallas_call | solution.py:63
  19.1 0.0 copy-start.1
  19.1 0.1 copy.14
  19.2 0.0 copy-start.2
  19.2 9.4 %all_to_all.122 = f32[32,1,640]{2,1,0:T(1,128)S(1)} all-to-all(f32[32,1,640]{2,1,0:T(1,128)S(1)} %copy.14), channel_id=1, replica_groups=mesh['gx'=4,'gy'=8] {'gx','gy'}, dimensions={0} | all-to-all | bytes 163840 | tf_op jit(solution)/shard_map/all_to_all | solution.py:552
  28.6 0.0 copy-done.4
  28.6 0.0 copy-done
  28.6 0.0 copy-done.1
  28.6 0.0 copy-done.2
  28.7 1.8 %shard_map.124 = (f32[8,3,16,128]{3,2,1,0:T(8,128)S(1)}, f32[3,16,128]{2,1,0:T(8,128)S(1)}, f32[3,16,128]{2,1,0:T(8,128)S(1)}, f32[8,3,16,128]{3,2,1,0:T(8,128)S...) custom-call(f32[32,640]{1,0:T(8,128)S(1)} %bitcast.46, f32[8,3,16,128]{3,2,1,0:T(8,128)S(1)} %get-tuple-element.62.refs_1_, ...), custom_call_target="tpu_custom_call" | custom-call | tf_op jit(solution)/shard_map/pallas_call | solution.py:63
  30.4 0.1 copy.15
  30.5 9.0 %all_to_all.123 = f32[32,1,384]{2,1,0:T(1,128)S(1)} all-to-all(f32[32,1,384]{2,1,0:T(1,128)S(1)} %copy.15), channel_id=1, replica_groups=mesh['gx'=4,'gy'=8] {'gx','gy'}, dimensions={0} | all-to-all | bytes 98304 | tf_op jit(solution)/shard_map/all_to_all | solution.py:552
  39.5 0.6 shard_map.125
  40.1 0.1 copy.16
  40.1 9.0 %all_to_all.124 = f32[32,1,384]{2,1,0:T(1,128)S(1)} all-to-all(f32[32,1,384]{2,1,0:T(1,128)S(1)} %copy.16), channel_id=1, replica_groups=mesh['gx'=4,'gy'=8] {'gx','gy'}, dimensions={0} | all-to-all | bytes 98304 | tf_op jit(solution)/shard_map/all_to_all | solution.py:552
  49.1 1.6 %shard_map.126 = (f32[8,3,16,128]{3,2,1,0:T(8,128)S(1)}, f32[8,3,16,128]{3,2,1,0:T(8,128)S(1)}, f32[400,128]{1,0:T(8,128)S(1)}, f32[32,384]{1,0:T(8,128)S(1)}) custom-call(f32[32,384]{1,0:T(8,128)S(1)} %bitcast.54, f32[8,3,16,128]{3,2,1,0:T(8,128)S(1)} %get-tuple-element.70.refs_1_, f32[400,128]{1,0:T(8,128)S(1)} %get-tuple-element.71.refs_2_, ...), custom_call_target="tpu_custom_call" | custom-call | tf_op jit(solution)/shard_map/pallas_call | solution.py:63
  50.7 0.1 copy.17
  50.8 9.0 %all_to_all.125 = f32[32,1,384]{2,1,0:T(1,128)S(1)} all-to-all(f32[32,1,384]{2,1,0:T(1,128)S(1)} %copy.17), channel_id=1, replica_groups=mesh['gx'=4,'gy'=8] {'gx','gy'}, dimensions={0} | all-to-all | bytes 98304 | tf_op jit(solution)/shard_map/all_to_all | solution.py:552
  59.8 0.6 shard_map.127
  60.4 0.1 copy.18
  60.4 9.0 %all_to_all.126 = f32[32,1,384]{2,1,0:T(1,128)S(1)} all-to-all(f32[32,1,384]{2,1,0:T(1,128)S(1)} %copy.18), channel_id=1, replica_groups=mesh['gx'=4,'gy'=8] {'gx','gy'}, dimensions={0} | all-to-all | bytes 98304 | tf_op jit(solution)/shard_map/all_to_all | solution.py:552
  69.4 1.6 %shard_map.128 = (f32[8,128]{1,0:T(8,128)S(1)}, f32[8,3,16,128]{3,2,1,0:T(8,128)S(1)}, f32[8,3,16,128]{3,2,1,0:T(8,128)S(1)}, f32[8,3,16,128]{3,2,1,0:T(8,128)S(...) custom-call(f32[32,384]{1,0:T(8,128)S(1)} %bitcast.56, ...), custom_call_target="tpu_custom_call" | custom-call | tf_op jit(solution)/shard_map/pallas_call | solution.py:63
  71.1 0.1 copy.19
  71.1 9.0 %all_to_all.127 = f32[32,1,384]{2,1,0:T(1,128)S(1)} all-to-all(f32[32,1,384]{2,1,0:T(1,128)S(1)} %copy.19), channel_id=1, replica_groups=mesh['gx'=4,'gy'=8] {'gx','gy'}, dimensions={0} | all-to-all | bytes 98304 | tf_op jit(solution)/shard_map/all_to_all | solution.py:552
  80.1 0.6 shard_map.129
  80.7 0.1 copy.20
  80.8 9.0 %all_to_all.128 = f32[32,1,384]{2,1,0:T(1,128)S(1)} all-to-all(f32[32,1,384]{2,1,0:T(1,128)S(1)} %copy.20), channel_id=1, replica_groups=mesh['gx'=4,'gy'=8] {'gx','gy'}, dimensions={0} | all-to-all | bytes 98304 | tf_op jit(solution)/shard_map/all_to_all | solution.py:552
  89.8 1.7 %shard_map.130 = (f32[8,128]{1,0:T(8,128)S(1)}, f32[8,3,16,128]{3,2,1,0:T(8,128)S(1)}, f32[8,3,16,128]{3,2,1,0:T(8,128)S(1)}, f32[8,3,16,128]{3,2,1,0:T(8,128)S(...) custom-call(f32[32,384]{1,0:T(8,128)S(1)} %bitcast.48, ...), custom_call_target="tpu_custom_call" | custom-call | tf_op jit(solution)/shard_map/pallas_call | solution.py:63
  91.5 0.1 copy.21
  91.5 9.0 %all_to_all.129 = f32[32,1,384]{2,1,0:T(1,128)S(1)} all-to-all(f32[32,1,384]{2,1,0:T(1,128)S(1)} %copy.21), channel_id=1, replica_groups=mesh['gx'=4,'gy'=8] {'gx','gy'}, dimensions={0} | all-to-all | bytes 98304 | tf_op jit(solution)/shard_map/all_to_all | solution.py:552
  100.5 0.6 shard_map.131
  101.1 0.1 copy.22
  101.2 9.0 %all_to_all.130 = f32[32,1,384]{2,1,0:T(1,128)S(1)} all-to-all(f32[32,1,384]{2,1,0:T(1,128)S(1)} %copy.22), channel_id=1, replica_groups=mesh['gx'=4,'gy'=8] {'gx','gy'}, dimensions={0} | all-to-all | bytes 98304 | tf_op jit(solution)/shard_map/all_to_all | solution.py:552
  110.2 0.0 copy-start.3
  110.2 0.7 shard_map.132
  110.9 8.8 %all_to_all.131 = f32[32,1,128]{2,1,0:T(1,128)S(1)} all-to-all(f32[32,1,128]{2,1,0:T(1,128)S(1)} %bitcast.67), channel_id=1, replica_groups=mesh['gx'=4,'gy'=8] {'gx','gy'}, dimensions={0} | all-to-all | bytes 32768 | tf_op jit(solution)/shard_map/all_to_all | solution.py:552
  119.8 0.0 copy-done.3
  119.8 1.0 shard_map.133
  (10 shorter events, 0.0 us)
Async XLA Ops:
  17.7 10.9 %copy-start.4 = (f32[8,3,16,128]{3,2,1,0:T(8,128)S(1)}, f32[8,3,16,128]{3,2,1,0:T(8,128)}, u32[]{:S(2)}) copy-start(f32[8,3,16,128]{3,2,1,0:T(8,128)} %refs_6_.3) | copy-start | bytes 589828
  17.7 10.9 %copy-start = (bf16[4,6,6,16,128]{4,3,2,1,0:T(8,128)(2,1)S(1)}, bf16[4,6,6,16,128]{4,3,2,1,0:T(8,128)(2,1)}, u32[]{:S(2)}) copy-start(bf16[4,6,6,16,128]{4,3,2,1,0:T(8,128)(2,1)} %inverse.1) | copy-start | bytes 1769476
  19.1 9.5 %copy-start.1 = (bf16[8,3,3,16,128]{4,3,2,1,0:T(8,128)(2,1)S(1)}, bf16[8,3,3,16,128]{4,3,2,1,0:T(8,128)(2,1)}, u32[]{:S(2)}) copy-start(bf16[8,3,3,16,128]{4,3,2,1,0:T(8,128)(2,1)} %refs_14_.3) | copy-start | bytes 884740
  19.2 9.4 %copy-start.2 = (bf16[6,8,16,128]{3,2,1,0:T(8,128)(2,1)S(1)}, bf16[6,8,16,128]{3,2,1,0:T(8,128)(2,1)}, u32[]{:S(2)}) copy-start(bf16[6,8,16,128]{3,2,1,0:T(8,128)(2,1)} %refs_15_.3) | copy-start | bytes 589828
  110.2 9.6 %copy-start.3 = (f32[8,3,16,128]{3,2,1,0:T(8,128)S(1)}, f32[8,3,16,128]{3,2,1,0:T(8,128)}, u32[]{:S(2)}) copy-start(f32[8,3,16,128]{3,2,1,0:T(8,128)} %guess.1) | copy-start | bytes 589828

commit v3 on v2

--- a/solution.py
+++ b/solution.py
@@ -70,6 +70,25 @@
     )(*held, *far)
 
 
+class Rows:
+    def __init__(self, ref, width):
+        self.ref, self.width = ref, width
+        self.devices = ref.shape[0] // width
+
+    def at(self, k, low=0, count=None):
+        count = self.devices - low if count is None else count
+        start = low * self.width + k
+        if self.width == 1 or count == 1:
+            return (slice(start, start + count), slice(None))
+        return (pl.ds(start, count, stride=self.width), slice(None))
+
+    def get(self, k, low=0, count=None):
+        return self.ref[self.at(k, low, count)]
+
+    def put(self, k, value, low=0):
+        self.ref[self.at(k, low, value.shape[0])] = value
+
+
 def iota(shape, dim):
     return lax.broadcasted_iota(jnp.int32, shape, dim)
 
@@ -91,11 +110,10 @@
     return jnp.where(rows == iota(rows.shape, 0), 1.0, 0.0).astype(BF16)
 
 
-def pack_slots(geo, block_ref, lane, packed_ref):
+def pack_slots(geo, rows, at_row, lane, packed_ref):
     packed_ref[...] = jnp.zeros_like(packed_ref)
-    start = lane // LANES * LANES
     for k, low, count in geo.pieces():
-        part = block_ref[low : low + count, start : start + LANES]
+        part = rows.get(at_row, low, count)
         shift = (k * geo.cap - lane) % LANES
         part = pltpu.roll(part, shift, 1) if shift else part
         at = iota(part.shape, 1)
@@ -103,31 +121,30 @@
         packed_ref[0:count, :] = jnp.where(mine, part, packed_ref[0:count, :])
 
 
-def unpack_slots(geo, packed, lane, block_ref):
+def unpack_slots(geo, packed, lane, rows):
     for k, low, count in geo.pieces():
         shift = (lane - k * geo.cap) % LANES
         part = pltpu.roll(packed, shift, 1) if shift else packed
         part = part[0:count]
         at = iota(part.shape, 1)
         mine = (at >= lane) & (at < lane + geo.cap)
-        block_ref[low : low + count, 0:LANES] = jnp.where(
-            mine, part, block_ref[low : low + count, 0:LANES]
-        )
+        rows.put(0, jnp.where(mine, part, rows.get(0, low, count)), low)
 
 
 def write_faces(geo, flux, send):
-    one, two, three = LANES, 2 * LANES, 3 * LANES
     if geo.devices > geo.faces + SUBS:
-        send[geo.faces + SUBS :, one:three] = jnp.zeros((geo.devices - geo.faces - SUBS, 2 * LANES), F32)
-    send[0 : geo.faces, one:two] = flux[pl.ds(geo.base(0), geo.faces, stride=geo.rows), :]
-    send[0 : geo.faces, two:three] = flux[pl.ds(geo.base(0) + geo.rows - 1, geo.faces, stride=geo.rows), :]
+        nothing = jnp.zeros((geo.devices - geo.faces - SUBS, LANES), F32)
+        send.put(1, nothing, geo.faces + SUBS)
+        send.put(2, nothing, geo.faces + SUBS)
+    send.put(1, flux[pl.ds(geo.base(0), geo.faces, stride=geo.rows), :])
+    send.put(2, flux[pl.ds(geo.base(0) + geo.rows - 1, geo.faces, stride=geo.rows), :])
     at = iota(geo.tile, 1) >> 1
     edges = jnp.zeros(geo.tile, F32)
     for j in range(geo.faces):
         turned = pltpu.roll(flux[geo.base(j) : geo.base(j) + geo.rows, :], 2 * j + 1, 1)
         edges = jnp.where(at == j, turned, edges)
-    send[geo.faces : geo.faces + SUBS, one:two] = edges[:SUBS]
-    send[geo.faces : geo.faces + SUBS, two:three] = edges[SUBS:]
+    send.put(1, edges[:SUBS], geo.faces)
+    send.put(2, edges[SUBS:], geo.faces)
 
 
 def write_flux(geo, mobility, vector, flux):
@@ -170,16 +187,17 @@
 
 def first_body(geo, *refs):
     far, refs = refs[:7], refs[7:]
-    (flux, send, rowp, lanep, spot_hot, hi, lo, inv_dev, inv_pos, turned, guess, mobility, well_in, well_out), refs = refs[:14], refs[14:]
-    cells, slots, inverse, wide, ints, packed, sems = refs
-    targets = (cells, slots, guess, mobility, inverse, well_in, well_out)
+    (flux, send, rowp, lanep, spot_hot, hi, lo, inv_dev, inv_pos, inverse_held, guess, mobility, well_in, well_out), refs = refs[:14], refs[14:]
+    cells, slots, wide, ints, packed, sems = refs
+    send = Rows(send, 3)
+    targets = (cells, slots, guess, mobility, inverse_held, well_in, well_out)
     copies = [pltpu.make_async_copy(source, target, sems.at[i]) for i, (source, target) in enumerate(zip(far, targets))]
     for copy in copies:
         copy.start()
     wide[...] = jnp.zeros_like(wide)
     copies[0].wait()
     wide[:, 0 : geo.cap] = cells[...] + 1
-    pack_slots(geo, wide, 0, ints)
+    pack_slots(geo, Rows(wide, 1), 0, 0, ints)
     index = ints[...] - 1
     rowp[...] = index >> 7
     lanep[...] = index & (LANES - 1)
@@ -189,7 +207,7 @@
     copies[3].wait()
     write_flux(geo, mobility, guess, flux)
     write_faces(geo, flux, send)
-    send[:, 0:LANES] = jnp.zeros((geo.devices, LANES), F32)
+    send.put(0, jnp.zeros((geo.devices, LANES), F32))
     packed[...] = jnp.zeros_like(packed)
 
     def finish(g, kept):
@@ -203,11 +221,8 @@
         row, lane = rowp[g : g + 1, :], lanep[g : g + 1, :]
         upper = jnp.where(row >= geo.half_rows, LANES, 0)
         spot_hot[:, g * LANES : (g + 1) * LANES] = one_hot(upper + lane, 2 * LANES)
-    copies[4].wait()
-    for w in range(geo.wells):
-        turned[w] = inverse[w].T
-    copies[5].wait()
-    copies[6].wait()
+    for copy in copies[4:]:
+        copy.wait()
 
 
 def slot_tables(geo, slot_ref, hi, lo, inv_dev, inv_pos, wide, packed):
@@ -215,7 +230,7 @@
     slots = wide[...] - 1
     hi[...] = slots >> 7
     lo[...] = slots & (LANES - 1)
-    pack_slots(geo, wide, 0, packed)
+    pack_slots(geo, Rows(wide, 1), 0, 0, packed)
     slots = packed[...] - 1
     slot_hi = slots >> 7
     slot_lo = slots & (LANES - 1)
@@ -240,8 +255,7 @@
     within = lax.rem(at, geo.n_gy)
     faces = jnp.full(shape, lax.axis_index(AXES), jnp.int32) < geo.faces
     up, down, count = geo.n_gy, geo.devices - geo.n_gy, geo.devices
-    one = came[:, LANES : 2 * LANES]
-    two = came[:, 2 * LANES : 3 * LANES]
+    one, two = came.get(1), came.get(2)
     after = jnp.where(at < down, pltpu.roll(one, down, 0), 0.0)
     before = jnp.where(at >= up, pltpu.roll(two, up, 0), 0.0)
 
@@ -250,8 +264,8 @@
         high = jnp.where(within < geo.n_gy - 1, pltpu.roll(pltpu.roll(block, LANES - 1, 1), count - 1, 0), 0.0)
         return jnp.where(even, high, low)
 
-    back[:, LANES : 2 * LANES] = jnp.where(faces, after, beside(one))
-    back[:, 2 * LANES : 3 * LANES] = jnp.where(faces, before, beside(two))
+    back.put(1, jnp.where(faces, after, beside(one)))
+    back.put(2, jnp.where(faces, before, beside(two)))
 
 
 def at_segments(geo, came, inv_dev, inv_pos, offset):
@@ -260,7 +274,7 @@
     position = inv_pos[...] + offset
     kept = jnp.zeros(shape, F32)
     for s in range(geo.devices):
-        found = take_lanes(spread(came[s : s + 1, 0:LANES], shape), position)
+        found = take_lanes(spread(came.get(0, s, 1), shape), position)
         kept = jnp.where(device == s, found, kept)
     return kept
 
@@ -274,40 +288,44 @@
     return kept
 
 
-def solve_segments(geo, rate, turned):
-    rate_t = rate.T
+def solve_segments(geo, rate, inverse):
+    shape = (geo.segs, LANES)
+    own = iota(shape, 0) == iota(shape, 1)
     rows = []
     for w in range(geo.wells):
-        rows.append(jnp.sum(turned[w] * rate_t[:, w : w + 1], axis=0, keepdims=True))
+        sums = jnp.sum(inverse[w] * rate[w : w + 1, :], axis=1, keepdims=True)
+        rows.append(jnp.sum(jnp.where(own, spread(sums, shape), 0.0), axis=0, keepdims=True))
     return rows
 
 
-def owner_first_body(geo, came, inv_dev, inv_pos, hi_ref, lo_ref, turned, well_in, well_out, back):
+def owner_first_body(geo, came, inv_dev, inv_pos, hi_ref, lo_ref, inverse_held, well_in, well_out, back):
+    came, back = Rows(came, 3), Rows(back, 5)
     hi, lo = hi_ref[...], lo_ref[...]
     rows_in = [[well_in[c : c + 1, w * LANES : (w + 1) * LANES] for w in range(geo.wells)] for c in range(3)]
     rows_out = [[well_out[c : c + 1, w * LANES : (w + 1) * LANES] for w in range(geo.wells)] for c in range(3)]
     rate = jnp.zeros((geo.wells, LANES), F32)
     for c in range(3):
         rate += jnp.concatenate(rows_in[c], axis=0) * at_segments(geo, came, inv_dev, inv_pos, c * geo.cap)
-    back[:, 0:LANES] = at_slots(geo, solve_segments(geo, rate, turned), hi, lo)
+    back.put(0, at_slots(geo, solve_segments(geo, rate, inverse_held), hi, lo))
     relay(geo, came, back)
     for place, rows in ((3, rows_in), (4, rows_out)):
         block = jnp.zeros((geo.devices, LANES), F32)
         for c in range(3):
             part = at_slots(geo, rows[c], hi, lo)
             block += pltpu.roll(part, c * geo.cap, 1) if c else part
-        back[:, place * LANES : (place + 1) * LANES] = block
-
-
-def owner_body(geo, came, inv_dev, inv_pos, hi_ref, lo_ref, turned, back, sums):
+        back.put(place, block)
+
+
+def owner_body(geo, came, inv_dev, inv_pos, hi_ref, lo_ref, inverse_held, back, sums):
+    came, back = Rows(came, 3), Rows(back, 3)
     rate = at_segments(geo, came, inv_dev, inv_pos, 0)
-    back[:, 0:LANES] = at_slots(geo, solve_segments(geo, rate, turned), hi_ref[...], lo_ref[...])
+    back.put(0, at_slots(geo, solve_segments(geo, rate, inverse_held), hi_ref[...], lo_ref[...]))
     relay(geo, came, back)
-    sums[...] = spread(jnp.sum(came[:, 0:LANES], axis=0, keepdims=True), sums.shape)
+    sums[...] = spread(jnp.sum(came.get(0), axis=0, keepdims=True), sums.shape)
 
 
 def scatter_terms(geo, came, coeff_out, rowp, spot_hot, packed, left, spots):
-    pack_slots(geo, came, 0, packed)
+    pack_slots(geo, came, 0, 0, packed)
     rate = packed[...]
     parts = []
     for c in range(3):
@@ -332,9 +350,7 @@
 
 def apply_operator(geo, came, vector, flux, diag, face, spots, store):
     at_row, at_lane = iota((SUBS, LANES), 0), iota(geo.tile, 1)
-    one, two, three = LANES, 2 * LANES, 3 * LANES
-    last = geo.faces + SUBS
-    edges = jnp.concatenate([came[geo.faces : last, one:two], came[geo.faces : last, two:three]], axis=0)
+    edges = jnp.concatenate([came.get(1, geo.faces, SUBS), came.get(2, geo.faces, SUBS)], axis=0)
     for z in range(geo.layers):
         f = [face[n, z].astype(F32) for n in range(6)]
         v = [vector[z, b] for b in range(3)]
@@ -342,9 +358,9 @@
             j = 3 * z + a
             base = geo.base(j)
             block = flux[base : base + geo.rows, :]
-            first = jnp.where(at_row == 0, spread(came[j : j + 1, two:three], at_row.shape), flux[base - 1 : base - 1 + SUBS, :])
+            first = jnp.where(at_row == 0, spread(came.get(2, j, 1), at_row.shape), flux[base - 1 : base - 1 + SUBS, :])
             under = jnp.concatenate([first, flux[base - 1 + SUBS : base - 1 + geo.rows, :]], axis=0)
-            final = jnp.where(at_row == SUBS - 1, spread(came[j : j + 1, one:two], at_row.shape), flux[base + 1 + SUBS : base + 1 + geo.rows, :])
+            final = jnp.where(at_row == SUBS - 1, spread(came.get(1, j, 1), at_row.shape), flux[base + 1 + SUBS : base + 1 + geo.rows, :])
             over = jnp.concatenate([flux[base + 1 : base + 1 + SUBS, :], final], axis=0)
             ends = pltpu.roll(edges, LANES - 1 - 2 * j, 1)
             left = jnp.where(at_lane == 0, ends, pltpu.roll(block, 1, 1))
@@ -366,13 +382,11 @@
         ahead[z, c] = block
 
     precondition(geo, inverse, lambda z, c: source[z, c], put)
-    write_flux(geo, mobility, ahead, flux)
-    write_faces(geo, flux, send)
     at = iota((1, LANES), 1)
     row = jnp.zeros((1, LANES), F32)
     for n, dot in enumerate(dots):
         row = jnp.where(at == geo.cap + n, spread(total(dot), (1, LANES)), row)
-    send[:, 0:LANES] = spread(row, (geo.devices, LANES))
+    send.put(0, spread(row, (geo.devices, LANES)))
     packed[...] = jnp.zeros_like(packed)
 
     def finish(g, kept):
@@ -382,6 +396,8 @@
         packed[g : g + 1, :] = jnp.sum(rate, axis=0, keepdims=True)
 
     gather_cells(geo, ahead, rowp, lanep, finish)
+    write_flux(geo, mobility, ahead, flux)
+    write_faces(geo, flux, send)
     unpack_slots(geo, packed[...], 0, send)
 
 
@@ -398,11 +414,13 @@
     outputs = take(n_out)
     following = take(3) if goes_on else take(1)
     packed, left, spots = take(3)
+    came = Rows(came, came.shape[0] // geo.devices)
     coeff_in, coeff_out, store, source, dots = rule(came, packed, inputs, outputs)
     scatter_terms(geo, came, coeff_out, rowp, spot_hot, packed, left, spots)
     apply_operator(geo, came, vector, flux_in, diag, face, spots, store)
     if goes_on:
         ahead, flux, send = following
+        send = Rows(send, 3)
         send_next(geo, source, *hats, rowp, lanep, coeff_in, dots, ahead, flux, send, packed)
     else:
         at = iota((1, LANES), 1)
@@ -426,9 +444,9 @@
     (right_side,) = inputs
     shadow, coeff_in, coeff_out = outputs
     for c in range(3):
-        pack_slots(geo, came, 3 * LANES + c * geo.cap, packed)
+        pack_slots(geo, came, 3, c * geo.cap, packed)
         coeff_in[c] = packed[...]
-        pack_slots(geo, came, 4 * LANES + c * geo.cap, packed)
+        pack_slots(geo, came, 4, c * geo.cap, packed)
         coeff_out[c] = packed[...]
     dots = zeros(geo, 1)
 
@@ -548,8 +566,9 @@
         copy.wait()
 
 
-def exchange(rows):
-    return lax.all_to_all(rows, AXES, split_axis=0, concat_axis=0, tiled=True)
+def exchange(geo, rows):
+    wide = rows.reshape(geo.devices, 1, rows.size // geo.devices)
+    return lax.all_to_all(wide, AXES, split_axis=0, concat_axis=0, tiled=True).reshape(rows.shape)
 
 
 def per_device(right_side, guess, diag, mobility, face, inverse, perf_cell, perf_slot, well_in, well_out, well_inverse):
@@ -558,22 +577,22 @@
     block = (geo.devices, LANES)
     packed = (geo.groups_pad, LANES)
     seg = (geo.wells, LANES)
-    wide = ((geo.devices, 3 * LANES), F32)
+    wide = ((3 * geo.devices, LANES), F32)
     small = ((SUBS, LANES), F32)
     vec = (geo.vector, F32)
     coeffs = ((3,) + packed, F32)
     sent = [vec, (geo.flux, F32), wide]
 
     table = (perf_cell.shape[1:], ints)
-    flux, send, rowp, lanep, spot_hot, hi, lo, inv_dev, inv_pos, turned, guess_held, mobility, well_in, well_out = call(
+    flux, send, rowp, lanep, spot_hot, hi, lo, inv_dev, inv_pos, inverse_held, guess_held, mobility, well_in, well_out = call(
         functools.partial(first_body, geo),
         [(geo.flux, F32), wide, (packed, ints), (packed, ints), ((2 * LANES, geo.slots), BF16), (block, ints), (block, ints),
          (seg, ints), (seg, ints), (well_inverse.shape, F32), vec, (mobility.shape, BF16), (well_in.shape, F32), (well_out.shape, F32)],
         [], far=[perf_cell[0], perf_slot[0], guess, mobility, well_inverse, well_in, well_out],
-        scratch=[pltpu.VMEM(*table), pltpu.VMEM(*table), pltpu.VMEM(well_inverse.shape, F32), pltpu.VMEM(block, ints),
+        scratch=[pltpu.VMEM(*table), pltpu.VMEM(*table), pltpu.VMEM(block, ints),
                  pltpu.VMEM(packed, ints), pltpu.VMEM((3,) + packed, F32), pltpu.SemaphoreType.DMA((7,))],
     )
-    owner_tables = [inv_dev, inv_pos, hi, lo, turned]
+    owner_tables = [inv_dev, inv_pos, hi, lo, inverse_held]
     scratch = [pltpu.VMEM(packed, F32), pltpu.VMEM((6 * geo.half_rows, geo.slots), BF16), pltpu.VMEM((3 * geo.tile_rows, LANES), F32)]
 
     def stage(rule, outs, came, vector, flux, inputs, goes_on=True):
@@ -590,13 +609,13 @@
         )
 
     def owner(send):
-        back, sums = call(functools.partial(owner_body, geo), [wide, small], [exchange(send)] + owner_tables)
-        return exchange(back), sums
+        back, sums = call(functools.partial(owner_body, geo), [wide, small], [exchange(geo, send)] + owner_tables)
+        return exchange(geo, back), sums
 
     (back,) = call(
-        functools.partial(owner_first_body, geo), [((geo.devices, 5 * LANES), F32)], [exchange(send)] + owner_tables + [well_in, well_out]
+        functools.partial(owner_first_body, geo), [((5 * geo.devices, LANES), F32)], [exchange(geo, send)] + owner_tables + [well_in, well_out]
     )
-    shadow, coeff_in, coeff_out, ahead, flux, send = stage(residual_rule, [vec, coeffs, coeffs], exchange(back), guess_held, flux, [right_side])
+    shadow, coeff_in, coeff_out, ahead, flux, send = stage(residual_rule, [vec, coeffs, coeffs], exchange(geo, back), guess_held, flux, [right_side])
     always = [coeff_in, coeff_out, shadow]
     came, sums = owner(send)
     rho, rho_at = sums, geo.cap
@@ -620,7 +639,7 @@
         )
         rho_at = 0
     return call(
-        functools.partial(finish_body, geo), [vec] * 2, [exchange(send), moved, half, response, guess, inverse],
+        functools.partial(finish_body, geo), [vec] * 2, [exchange(geo, send), moved, half, response, guess, inverse],
         scratch=[pltpu.VMEM(*vec), pltpu.VMEM(*vec), pltpu.SemaphoreType.DMA((2, geo.layers))], out_far=True,
     )
 

time: 121 us -> 119 us (0.983)
  no operation moved by 1% of the time
where the time goes in v3:
time: 119 us
  blocking collectives  105 us (88%)
  Pallas kernels  13.8 us (12%)
    all_to_all x11, blocking collectives, exchange(): lax.all_to_all(wide, AXES, split_axis=0, concat_axis=0, tiled=True)  105 us
    pallas_call x12, Pallas kernels, call(): pl.pallas_call(body, out_shape=tuple(shapes), in_specs=[HELD] * len(held)...  13.8 us

profile of v3, /device:TPU:0, one launch (start us, length us, event | category | flops | bytes accessed | tf_op | source)
XLA Modules:
  0.0 119.0 jit_solution(1087851567886571718)
XLA Ops:
  0.6 0.0 copy-start.2
  0.6 0.0 copy-start.4
  0.7 2.4 %shard_map.122 = (f32[400,128]{1,0:T(8,128)S(1)}, f32[96,128]{1,0:T(8,128)S(1)}, s32[16,128]{1,0:T(8,128)S(1)}, s32[16,128]{1,0:T(8,128)S(1)}, bf16[256,1408]{1,...) custom-call(s32[32,40]{1,0:T(8,128)} %bitcast.48, ...), custom_call_target="tpu_custom_call" | custom-call | tf_op jit(solution)/shard_map/pallas_call | solution.py:63
  3.1 0.0 copy-start
  3.1 14.4 %all_to_all.55 = f32[32,1,384]{2,1,0:T(1,128)S(1)} all-to-all(f32[32,1,384]{2,1,0:T(1,128)S(1)} %bitcast.39), channel_id=1, replica_groups=mesh['gx'=4,'gy'=8] {'gx','gy'}, dimensions={0} | all-to-all | bytes 98304 | tf_op jit(solution)/shard_map/all_to_all | solution.py:571
  17.6 0.0 copy-start.1
  17.6 1.3 %shard_map.123 = f32[160,128]{1,0:T(8,128)S(1)} custom-call(f32[96,128]{1,0:T(8,128)S(1)} %bitcast.30, s32[8,128]{1,0:T(8,128)S(1)} %get-tuple-element.55.inv_dev, s32[8,128]{1,0:T(8,128)S(1)} %get-tuple-element.56.inv_pos, s32[32,128]{1,0:T(8,128)S(1)} %get-tuple-element.57.hi_ref, s32[32,128]{1,0:T(8,128)S(1)} %get-tuple-element.58.lo_ref, ...), custom_call_target="tpu_custom_call" | custom-call | tf_op jit(solution)/shard_map/pallas_call | solution.py:63
  18.9 9.2 %all_to_all.56 = f32[32,1,640]{2,1,0:T(1,128)S(1)} all-to-all(f32[32,1,640]{2,1,0:T(1,128)S(1)} %bitcast.27), channel_id=1, replica_groups=mesh['gx'=4,'gy'=8] {'gx','gy'}, dimensions={0} | all-to-all | bytes 163840 | tf_op jit(solution)/shard_map/all_to_all | solution.py:571
  28.1 0.0 copy-done.2
  28.1 0.0 copy-done.4
  28.1 0.0 copy-done
  28.1 0.0 copy-done.1
  28.1 1.7 %shard_map.124 = (f32[8,3,16,128]{3,2,1,0:T(8,128)S(1)}, f32[3,16,128]{2,1,0:T(8,128)S(1)}, f32[3,16,128]{2,1,0:T(8,128)S(1)}, f32[8,3,16,128]{3,2,1,0:T(8,128)S...) custom-call(f32[160,128]{1,0:T(8,128)S(1)} %bitcast.26, f32[8,3,16,128]{3,2,1,0:T(8,128)S(1)} %get-tuple-element.62.refs_1_, ...), custom_call_target="tpu_custom_call" | custom-call | tf_op jit(solution)/shard_map/pallas_call | solution.py:63
  29.8 9.0 %all_to_all.57 = f32[32,1,384]{2,1,0:T(1,128)S(1)} all-to-all(f32[32,1,384]{2,1,0:T(1,128)S(1)} %bitcast.41), channel_id=1, replica_groups=mesh['gx'=4,'gy'=8] {'gx','gy'}, dimensions={0} | all-to-all | bytes 98304 | tf_op jit(solution)/shard_map/all_to_all | solution.py:571
  38.8 0.4 shard_map.125
  39.3 9.0 %all_to_all.58 = f32[32,1,384]{2,1,0:T(1,128)S(1)} all-to-all(f32[32,1,384]{2,1,0:T(1,128)S(1)} %bitcast.44), channel_id=1, replica_groups=mesh['gx'=4,'gy'=8] {'gx','gy'}, dimensions={0} | all-to-all | bytes 98304 | tf_op jit(solution)/shard_map/all_to_all | solution.py:571
  48.3 1.5 %shard_map.126 = (f32[8,3,16,128]{3,2,1,0:T(8,128)S(1)}, f32[8,3,16,128]{3,2,1,0:T(8,128)S(1)}, f32[400,128]{1,0:T(8,128)S(1)}, f32[96,128]{1,0:T(8,128)S(1)}) custom-call(f32[96,128]{1,0:T(8,128)S(1)} %bitcast.34, f32[8,3,16,128]{3,2,1,0:T(8,128)S(1)} %get-tuple-element.70.refs_1_, f32[400,128]{1,0:T(8,128)S(1)} %get-tuple-element.71.refs_2_, ...), custom_call_target="tpu_custom_call" | custom-call | tf_op jit(solution)/shard_map/pallas_call | solution.py:63
  49.8 9.0 %all_to_all.59 = f32[32,1,384]{2,1,0:T(1,128)S(1)} all-to-all(f32[32,1,384]{2,1,0:T(1,128)S(1)} %bitcast.43), channel_id=1, replica_groups=mesh['gx'=4,'gy'=8] {'gx','gy'}, dimensions={0} | all-to-all | bytes 98304 | tf_op jit(solution)/shard_map/all_to_all | solution.py:571
  58.8 0.4 shard_map.127
  59.3 9.0 %all_to_all.60 = f32[32,1,384]{2,1,0:T(1,128)S(1)} all-to-all(f32[32,1,384]{2,1,0:T(1,128)S(1)} %bitcast.45), channel_id=1, replica_groups=mesh['gx'=4,'gy'=8] {'gx','gy'}, dimensions={0} | all-to-all | bytes 98304 | tf_op jit(solution)/shard_map/all_to_all | solution.py:571
  68.3 1.6 %shard_map.128 = (f32[8,128]{1,0:T(8,128)S(1)}, f32[8,3,16,128]{3,2,1,0:T(8,128)S(1)}, f32[8,3,16,128]{3,2,1,0:T(8,128)S(1)}, f32[8,3,16,128]{3,2,1,0:T(8,128)S(...) custom-call(f32[96,128]{1,0:T(8,128)S(1)} %bitcast.36, ...), custom_call_target="tpu_custom_call" | custom-call | tf_op jit(solution)/shard_map/pallas_call | solution.py:63
  69.9 9.0 %all_to_all.61 = f32[32,1,384]{2,1,0:T(1,128)S(1)} all-to-all(f32[32,1,384]{2,1,0:T(1,128)S(1)} %bitcast.40), channel_id=1, replica_groups=mesh['gx'=4,'gy'=8] {'gx','gy'}, dimensions={0} | all-to-all | bytes 98304 | tf_op jit(solution)/shard_map/all_to_all | solution.py:571
  78.9 0.4 shard_map.129
  79.3 9.0 %all_to_all.62 = f32[32,1,384]{2,1,0:T(1,128)S(1)} all-to-all(f32[32,1,384]{2,1,0:T(1,128)S(1)} %bitcast.46), channel_id=1, replica_groups=mesh['gx'=4,'gy'=8] {'gx','gy'}, dimensions={0} | all-to-all | bytes 98304 | tf_op jit(solution)/shard_map/all_to_all | solution.py:571
  88.3 1.6 %shard_map.130 = (f32[8,128]{1,0:T(8,128)S(1)}, f32[8,3,16,128]{3,2,1,0:T(8,128)S(1)}, f32[8,3,16,128]{3,2,1,0:T(8,128)S(1)}, f32[8,3,16,128]{3,2,1,0:T(8,128)S(...) custom-call(f32[96,128]{1,0:T(8,128)S(1)} %bitcast.28, ...), custom_call_target="tpu_custom_call" | custom-call | tf_op jit(solution)/shard_map/pallas_call | solution.py:63
  90.0 9.0 %all_to_all.63 = f32[32,1,384]{2,1,0:T(1,128)S(1)} all-to-all(f32[32,1,384]{2,1,0:T(1,128)S(1)} %bitcast.38), channel_id=1, replica_groups=mesh['gx'=4,'gy'=8] {'gx','gy'}, dimensions={0} | all-to-all | bytes 98304 | tf_op jit(solution)/shard_map/all_to_all | solution.py:571
  99.0 0.4 shard_map.131
  99.4 9.0 %all_to_all.64 = f32[32,1,384]{2,1,0:T(1,128)S(1)} all-to-all(f32[32,1,384]{2,1,0:T(1,128)S(1)} %bitcast.42), channel_id=1, replica_groups=mesh['gx'=4,'gy'=8] {'gx','gy'}, dimensions={0} | all-to-all | bytes 98304 | tf_op jit(solution)/shard_map/all_to_all | solution.py:571
  108.4 0.0 copy-start.3
  108.4 0.7 shard_map.132
  109.2 8.9 %all_to_all.65 = f32[32,1,128]{2,1,0:T(1,128)S(1)} all-to-all(f32[32,1,128]{2,1,0:T(1,128)S(1)} %bitcast.47), channel_id=1, replica_groups=mesh['gx'=4,'gy'=8] {'gx','gy'}, dimensions={0} | all-to-all | bytes 32768 | tf_op jit(solution)/shard_map/all_to_all | solution.py:571
  118.0 0.0 copy-done.3
  118.0 1.0 shard_map.133
Async XLA Ops:
  0.6 27.5 %copy-start.2 = (bf16[6,8,16,128]{3,2,1,0:T(8,128)(2,1)S(1)}, bf16[6,8,16,128]{3,2,1,0:T(8,128)(2,1)}, u32[]{:S(2)}) copy-start(bf16[6,8,16,128]{3,2,1,0:T(8,128)(2,1)} %refs_15_.3) | copy-start | bytes 589828
  0.6 27.5 %copy-start.4 = (f32[8,3,16,128]{3,2,1,0:T(8,128)S(1)}, f32[8,3,16,128]{3,2,1,0:T(8,128)}, u32[]{:S(2)}) copy-start(f32[8,3,16,128]{3,2,1,0:T(8,128)} %refs_6_.3) | copy-start | bytes 589828
  3.1 25.0 %copy-start = (bf16[4,6,6,16,128]{4,3,2,1,0:T(8,128)(2,1)S(1)}, bf16[4,6,6,16,128]{4,3,2,1,0:T(8,128)(2,1)}, u32[]{:S(2)}) copy-start(bf16[4,6,6,16,128]{4,3,2,1,0:T(8,128)(2,1)} %inverse.1) | copy-start | bytes 1769476
  17.6 10.5 %copy-start.1 = (bf16[8,3,3,16,128]{4,3,2,1,0:T(8,128)(2,1)S(1)}, bf16[8,3,3,16,128]{4,3,2,1,0:T(8,128)(2,1)}, u32[]{:S(2)}) copy-start(bf16[8,3,3,16,128]{4,3,2,1,0:T(8,128)(2,1)} %refs_14_.3) | copy-start | bytes 884740
  108.4 9.6 %copy-start.3 = (f32[8,3,16,128]{3,2,1,0:T(8,128)S(1)}, f32[8,3,16,128]{3,2,1,0:T(8,128)}, u32[]{:S(2)}) copy-start(f32[8,3,16,128]{3,2,1,0:T(8,128)} %guess.1) | copy-start | bytes 589828

commit v4 on v3

--- a/solution.py
+++ b/solution.py
@@ -192,8 +192,8 @@
     send = Rows(send, 3)
     targets = (cells, slots, guess, mobility, inverse_held, well_in, well_out)
     copies = [pltpu.make_async_copy(source, target, sems.at[i]) for i, (source, target) in enumerate(zip(far, targets))]
-    for copy in copies:
-        copy.start()
+    for i in (0, 2, 3, 1, 4, 5, 6):
+        copies[i].start()
     wide[...] = jnp.zeros_like(wide)
     copies[0].wait()
     wide[:, 0 : geo.cap] = cells[...] + 1
@@ -203,6 +203,10 @@
     lanep[...] = index & (LANES - 1)
     copies[1].wait()
     slot_tables(geo, slots, hi, lo, inv_dev, inv_pos, wide, ints)
+    for g in range(geo.groups):
+        row, lane = rowp[g : g + 1, :], lanep[g : g + 1, :]
+        upper = jnp.where(row >= geo.half_rows, LANES, 0)
+        spot_hot[:, g * LANES : (g + 1) * LANES] = one_hot(upper + lane, 2 * LANES)
     copies[2].wait()
     copies[3].wait()
     write_flux(geo, mobility, guess, flux)
@@ -217,10 +221,6 @@
     gather_cells(geo, guess, rowp, lanep, finish)
     for c in range(3):
         unpack_slots(geo, packed[c], c * geo.cap, send)
-    for g in range(geo.groups):
-        row, lane = rowp[g : g + 1, :], lanep[g : g + 1, :]
-        upper = jnp.where(row >= geo.half_rows, LANES, 0)
-        spot_hot[:, g * LANES : (g + 1) * LANES] = one_hot(upper + lane, 2 * LANES)
     for copy in copies[4:]:
         copy.wait()
 

time: 119 us -> 119 us (level)
  no operation moved by 1% of the time
where the time goes in v4:
time: 119 us
  blocking collectives  105 us (88%)
  Pallas kernels  13.7 us (12%)
    all_to_all x11, blocking collectives, exchange(): lax.all_to_all(wide, AXES, split_axis=0, concat_axis=0, tiled=True)  105 us
    pallas_call x12, Pallas kernels, call(): pl.pallas_call(body, out_shape=tuple(shapes), in_specs=[HELD] * len(held)...  13.7 us

profile of v4, /device:TPU:0, one launch (start us, length us, event | category | flops | bytes accessed | tf_op | source)
XLA Modules:
  0.0 118.9 jit_solution(18404017693253904385)
XLA Ops:
  0.6 0.0 copy-start.2
  0.6 0.0 copy-start.4
  0.7 2.3 %shard_map.122 = (f32[400,128]{1,0:T(8,128)S(1)}, f32[96,128]{1,0:T(8,128)S(1)}, s32[16,128]{1,0:T(8,128)S(1)}, s32[16,128]{1,0:T(8,128)S(1)}, bf16[256,1408]{1,...) custom-call(s32[32,40]{1,0:T(8,128)} %bitcast.48, ...), custom_call_target="tpu_custom_call" | custom-call | tf_op jit(solution)/shard_map/pallas_call | solution.py:63
  3.0 0.0 copy-start
  3.0 14.4 %all_to_all.55 = f32[32,1,384]{2,1,0:T(1,128)S(1)} all-to-all(f32[32,1,384]{2,1,0:T(1,128)S(1)} %bitcast.39), channel_id=1, replica_groups=mesh['gx'=4,'gy'=8] {'gx','gy'}, dimensions={0} | all-to-all | bytes 98304 | tf_op jit(solution)/shard_map/all_to_all | solution.py:571
  17.5 0.0 copy-start.1
  17.5 1.3 %shard_map.123 = f32[160,128]{1,0:T(8,128)S(1)} custom-call(f32[96,128]{1,0:T(8,128)S(1)} %bitcast.30, s32[8,128]{1,0:T(8,128)S(1)} %get-tuple-element.55.inv_dev, s32[8,128]{1,0:T(8,128)S(1)} %get-tuple-element.56.inv_pos, s32[32,128]{1,0:T(8,128)S(1)} %get-tuple-element.57.hi_ref, s32[32,128]{1,0:T(8,128)S(1)} %get-tuple-element.58.lo_ref, ...), custom_call_target="tpu_custom_call" | custom-call | tf_op jit(solution)/shard_map/pallas_call | solution.py:63
  18.8 9.2 %all_to_all.56 = f32[32,1,640]{2,1,0:T(1,128)S(1)} all-to-all(f32[32,1,640]{2,1,0:T(1,128)S(1)} %bitcast.27), channel_id=1, replica_groups=mesh['gx'=4,'gy'=8] {'gx','gy'}, dimensions={0} | all-to-all | bytes 163840 | tf_op jit(solution)/shard_map/all_to_all | solution.py:571
  28.0 0.0 copy-done.2
  28.0 0.0 copy-done.4
  28.0 0.0 copy-done
  28.0 0.0 copy-done.1
  28.0 1.7 %shard_map.124 = (f32[8,3,16,128]{3,2,1,0:T(8,128)S(1)}, f32[3,16,128]{2,1,0:T(8,128)S(1)}, f32[3,16,128]{2,1,0:T(8,128)S(1)}, f32[8,3,16,128]{3,2,1,0:T(8,128)S...) custom-call(f32[160,128]{1,0:T(8,128)S(1)} %bitcast.26, f32[8,3,16,128]{3,2,1,0:T(8,128)S(1)} %get-tuple-element.62.refs_1_, ...), custom_call_target="tpu_custom_call" | custom-call | tf_op jit(solution)/shard_map/pallas_call | solution.py:63
  29.7 9.0 %all_to_all.57 = f32[32,1,384]{2,1,0:T(1,128)S(1)} all-to-all(f32[32,1,384]{2,1,0:T(1,128)S(1)} %bitcast.41), channel_id=1, replica_groups=mesh['gx'=4,'gy'=8] {'gx','gy'}, dimensions={0} | all-to-all | bytes 98304 | tf_op jit(solution)/shard_map/all_to_all | solution.py:571
  38.7 0.4 shard_map.125
  39.2 9.0 %all_to_all.58 = f32[32,1,384]{2,1,0:T(1,128)S(1)} all-to-all(f32[32,1,384]{2,1,0:T(1,128)S(1)} %bitcast.44), channel_id=1, replica_groups=mesh['gx'=4,'gy'=8] {'gx','gy'}, dimensions={0} | all-to-all | bytes 98304 | tf_op jit(solution)/shard_map/all_to_all | solution.py:571
  48.2 1.5 %shard_map.126 = (f32[8,3,16,128]{3,2,1,0:T(8,128)S(1)}, f32[8,3,16,128]{3,2,1,0:T(8,128)S(1)}, f32[400,128]{1,0:T(8,128)S(1)}, f32[96,128]{1,0:T(8,128)S(1)}) custom-call(f32[96,128]{1,0:T(8,128)S(1)} %bitcast.34, f32[8,3,16,128]{3,2,1,0:T(8,128)S(1)} %get-tuple-element.70.refs_1_, f32[400,128]{1,0:T(8,128)S(1)} %get-tuple-element.71.refs_2_, ...), custom_call_target="tpu_custom_call" | custom-call | tf_op jit(solution)/shard_map/pallas_call | solution.py:63
  49.7 9.0 %all_to_all.59 = f32[32,1,384]{2,1,0:T(1,128)S(1)} all-to-all(f32[32,1,384]{2,1,0:T(1,128)S(1)} %bitcast.43), channel_id=1, replica_groups=mesh['gx'=4,'gy'=8] {'gx','gy'}, dimensions={0} | all-to-all | bytes 98304 | tf_op jit(solution)/shard_map/all_to_all | solution.py:571
  58.7 0.4 shard_map.127
  59.2 9.0 %all_to_all.60 = f32[32,1,384]{2,1,0:T(1,128)S(1)} all-to-all(f32[32,1,384]{2,1,0:T(1,128)S(1)} %bitcast.45), channel_id=1, replica_groups=mesh['gx'=4,'gy'=8] {'gx','gy'}, dimensions={0} | all-to-all | bytes 98304 | tf_op jit(solution)/shard_map/all_to_all | solution.py:571
  68.2 1.6 %shard_map.128 = (f32[8,128]{1,0:T(8,128)S(1)}, f32[8,3,16,128]{3,2,1,0:T(8,128)S(1)}, f32[8,3,16,128]{3,2,1,0:T(8,128)S(1)}, f32[8,3,16,128]{3,2,1,0:T(8,128)S(...) custom-call(f32[96,128]{1,0:T(8,128)S(1)} %bitcast.36, ...), custom_call_target="tpu_custom_call" | custom-call | tf_op jit(solution)/shard_map/pallas_call | solution.py:63
  69.8 9.0 %all_to_all.61 = f32[32,1,384]{2,1,0:T(1,128)S(1)} all-to-all(f32[32,1,384]{2,1,0:T(1,128)S(1)} %bitcast.40), channel_id=1, replica_groups=mesh['gx'=4,'gy'=8] {'gx','gy'}, dimensions={0} | all-to-all | bytes 98304 | tf_op jit(solution)/shard_map/all_to_all | solution.py:571
  78.8 0.4 shard_map.129
  79.2 9.0 %all_to_all.62 = f32[32,1,384]{2,1,0:T(1,128)S(1)} all-to-all(f32[32,1,384]{2,1,0:T(1,128)S(1)} %bitcast.46), channel_id=1, replica_groups=mesh['gx'=4,'gy'=8] {'gx','gy'}, dimensions={0} | all-to-all | bytes 98304 | tf_op jit(solution)/shard_map/all_to_all | solution.py:571
  88.2 1.6 %shard_map.130 = (f32[8,128]{1,0:T(8,128)S(1)}, f32[8,3,16,128]{3,2,1,0:T(8,128)S(1)}, f32[8,3,16,128]{3,2,1,0:T(8,128)S(1)}, f32[8,3,16,128]{3,2,1,0:T(8,128)S(...) custom-call(f32[96,128]{1,0:T(8,128)S(1)} %bitcast.28, ...), custom_call_target="tpu_custom_call" | custom-call | tf_op jit(solution)/shard_map/pallas_call | solution.py:63
  89.9 9.0 %all_to_all.63 = f32[32,1,384]{2,1,0:T(1,128)S(1)} all-to-all(f32[32,1,384]{2,1,0:T(1,128)S(1)} %bitcast.38), channel_id=1, replica_groups=mesh['gx'=4,'gy'=8] {'gx','gy'}, dimensions={0} | all-to-all | bytes 98304 | tf_op jit(solution)/shard_map/all_to_all | solution.py:571
  98.9 0.4 shard_map.131
  99.3 9.0 %all_to_all.64 = f32[32,1,384]{2,1,0:T(1,128)S(1)} all-to-all(f32[32,1,384]{2,1,0:T(1,128)S(1)} %bitcast.42), channel_id=1, replica_groups=mesh['gx'=4,'gy'=8] {'gx','gy'}, dimensions={0} | all-to-all | bytes 98304 | tf_op jit(solution)/shard_map/all_to_all | solution.py:571
  108.3 0.0 copy-start.3
  108.3 0.7 shard_map.132
  109.1 8.9 %all_to_all.65 = f32[32,1,128]{2,1,0:T(1,128)S(1)} all-to-all(f32[32,1,128]{2,1,0:T(1,128)S(1)} %bitcast.47), channel_id=1, replica_groups=mesh['gx'=4,'gy'=8] {'gx','gy'}, dimensions={0} | all-to-all | bytes 32768 | tf_op jit(solution)/shard_map/all_to_all | solution.py:571
  117.9 0.0 copy-done.3
  117.9 1.0 shard_map.133
Async XLA Ops:
  0.6 27.4 %copy-start.2 = (bf16[6,8,16,128]{3,2,1,0:T(8,128)(2,1)S(1)}, bf16[6,8,16,128]{3,2,1,0:T(8,128)(2,1)}, u32[]{:S(2)}) copy-start(bf16[6,8,16,128]{3,2,1,0:T(8,128)(2,1)} %refs_15_.3) | copy-start | bytes 589828
  0.6 27.4 %copy-start.4 = (f32[8,3,16,128]{3,2,1,0:T(8,128)S(1)}, f32[8,3,16,128]{3,2,1,0:T(8,128)}, u32[]{:S(2)}) copy-start(f32[8,3,16,128]{3,2,1,0:T(8,128)} %refs_6_.3) | copy-start | bytes 589828
  3.0 25.0 %copy-start = (bf16[4,6,6,16,128]{4,3,2,1,0:T(8,128)(2,1)S(1)}, bf16[4,6,6,16,128]{4,3,2,1,0:T(8,128)(2,1)}, u32[]{:S(2)}) copy-start(bf16[4,6,6,16,128]{4,3,2,1,0:T(8,128)(2,1)} %inverse.1) | copy-start | bytes 1769476
  17.5 10.5 %copy-start.1 = (bf16[8,3,3,16,128]{4,3,2,1,0:T(8,128)(2,1)S(1)}, bf16[8,3,3,16,128]{4,3,2,1,0:T(8,128)(2,1)}, u32[]{:S(2)}) copy-start(bf16[8,3,3,16,128]{4,3,2,1,0:T(8,128)(2,1)} %refs_14_.3) | copy-start | bytes 884740
  108.3 9.6 %copy-start.3 = (f32[8,3,16,128]{3,2,1,0:T(8,128)S(1)}, f32[8,3,16,128]{3,2,1,0:T(8,128)}, u32[]{:S(2)}) copy-start(f32[8,3,16,128]{3,2,1,0:T(8,128)} %guess.1) | copy-start | bytes 589828

commit v5 on v4

--- a/solution.py
+++ b/solution.py
@@ -272,11 +272,11 @@
     shape = (geo.wells, LANES)
     device = inv_dev[...]
     position = inv_pos[...] + offset
-    kept = jnp.zeros(shape, F32)
+    kept = [jnp.zeros(shape, F32) for _ in range(4)]
     for s in range(geo.devices):
         found = take_lanes(spread(came.get(0, s, 1), shape), position)
-        kept = jnp.where(device == s, found, kept)
-    return kept
+        kept[s % 4] = jnp.where(device == s, found, kept[s % 4])
+    return (kept[0] + kept[1]) + (kept[2] + kept[3])
 
 
 def at_slots(geo, rows, hi, lo):
@@ -552,8 +552,8 @@
 
     for z, c in geo.tiles():
         residual[z, c] = half[z, c] - smoothing * response[z, c]
-        if c + 1 == geo.comps:
-            leave(residual, residual_out, z, sems.at[0, z])
+    copies.append(pltpu.make_async_copy(residual, residual_out, sems.at[0, 0]))
+    copies[-1].start()
 
     def put(z, c, block):
         solution[z, c] = guess[z, c] + block

time: 119 us -> 119 us (level)
  no operation moved by 1% of the time
where the time goes in v5:
time: 119 us
  blocking collectives  105 us (88%)
  Pallas kernels  13.7 us (12%)
    all_to_all x11, blocking collectives, exchange(): lax.all_to_all(wide, AXES, split_axis=0, concat_axis=0, tiled=True)  105 us
    pallas_call x12, Pallas kernels, call(): pl.pallas_call(body, out_shape=tuple(shapes), in_specs=[HELD] * len(held)...  13.7 us

profile of v5, /device:TPU:0, one launch (start us, length us, event | category | flops | bytes accessed | tf_op | source)
XLA Modules:
  0.0 119.0 jit_solution(5228117491752237210)
XLA Ops:
  0.6 0.0 copy-start.2
  0.6 0.0 copy-start.4
  0.7 2.3 %shard_map.122 = (f32[400,128]{1,0:T(8,128)S(1)}, f32[96,128]{1,0:T(8,128)S(1)}, s32[16,128]{1,0:T(8,128)S(1)}, s32[16,128]{1,0:T(8,128)S(1)}, bf16[256,1408]{1,...) custom-call(s32[32,40]{1,0:T(8,128)} %bitcast.48, ...), custom_call_target="tpu_custom_call" | custom-call | tf_op jit(solution)/shard_map/pallas_call | solution.py:63
  3.0 0.0 copy-start
  3.0 14.4 %all_to_all.55 = f32[32,1,384]{2,1,0:T(1,128)S(1)} all-to-all(f32[32,1,384]{2,1,0:T(1,128)S(1)} %bitcast.39), channel_id=1, replica_groups=mesh['gx'=4,'gy'=8] {'gx','gy'}, dimensions={0} | all-to-all | bytes 98304 | tf_op jit(solution)/shard_map/all_to_all | solution.py:571
  17.5 0.0 copy-start.1
  17.5 1.3 %shard_map.123 = f32[160,128]{1,0:T(8,128)S(1)} custom-call(f32[96,128]{1,0:T(8,128)S(1)} %bitcast.30, s32[8,128]{1,0:T(8,128)S(1)} %get-tuple-element.55.inv_dev, s32[8,128]{1,0:T(8,128)S(1)} %get-tuple-element.56.inv_pos, s32[32,128]{1,0:T(8,128)S(1)} %get-tuple-element.57.hi_ref, s32[32,128]{1,0:T(8,128)S(1)} %get-tuple-element.58.lo_ref, ...), custom_call_target="tpu_custom_call" | custom-call | tf_op jit(solution)/shard_map/pallas_call | solution.py:63
  18.8 9.2 %all_to_all.56 = f32[32,1,640]{2,1,0:T(1,128)S(1)} all-to-all(f32[32,1,640]{2,1,0:T(1,128)S(1)} %bitcast.27), channel_id=1, replica_groups=mesh['gx'=4,'gy'=8] {'gx','gy'}, dimensions={0} | all-to-all | bytes 163840 | tf_op jit(solution)/shard_map/all_to_all | solution.py:571
  28.0 0.0 copy-done.2
  28.0 0.0 copy-done.4
  28.0 0.0 copy-done
  28.0 0.0 copy-done.1
  28.0 1.7 %shard_map.124 = (f32[8,3,16,128]{3,2,1,0:T(8,128)S(1)}, f32[3,16,128]{2,1,0:T(8,128)S(1)}, f32[3,16,128]{2,1,0:T(8,128)S(1)}, f32[8,3,16,128]{3,2,1,0:T(8,128)S...) custom-call(f32[160,128]{1,0:T(8,128)S(1)} %bitcast.26, f32[8,3,16,128]{3,2,1,0:T(8,128)S(1)} %get-tuple-element.62.refs_1_, ...), custom_call_target="tpu_custom_call" | custom-call | tf_op jit(solution)/shard_map/pallas_call | solution.py:63
  29.8 9.0 %all_to_all.57 = f32[32,1,384]{2,1,0:T(1,128)S(1)} all-to-all(f32[32,1,384]{2,1,0:T(1,128)S(1)} %bitcast.41), channel_id=1, replica_groups=mesh['gx'=4,'gy'=8] {'gx','gy'}, dimensions={0} | all-to-all | bytes 98304 | tf_op jit(solution)/shard_map/all_to_all | solution.py:571
  38.8 0.5 shard_map.125
  39.2 9.0 %all_to_all.58 = f32[32,1,384]{2,1,0:T(1,128)S(1)} all-to-all(f32[32,1,384]{2,1,0:T(1,128)S(1)} %bitcast.44), channel_id=1, replica_groups=mesh['gx'=4,'gy'=8] {'gx','gy'}, dimensions={0} | all-to-all | bytes 98304 | tf_op jit(solution)/shard_map/all_to_all | solution.py:571
  48.2 1.5 %shard_map.126 = (f32[8,3,16,128]{3,2,1,0:T(8,128)S(1)}, f32[8,3,16,128]{3,2,1,0:T(8,128)S(1)}, f32[400,128]{1,0:T(8,128)S(1)}, f32[96,128]{1,0:T(8,128)S(1)}) custom-call(f32[96,128]{1,0:T(8,128)S(1)} %bitcast.34, f32[8,3,16,128]{3,2,1,0:T(8,128)S(1)} %get-tuple-element.70.refs_1_, f32[400,128]{1,0:T(8,128)S(1)} %get-tuple-element.71.refs_2_, ...), custom_call_target="tpu_custom_call" | custom-call | tf_op jit(solution)/shard_map/pallas_call | solution.py:63
  49.8 9.0 %all_to_all.59 = f32[32,1,384]{2,1,0:T(1,128)S(1)} all-to-all(f32[32,1,384]{2,1,0:T(1,128)S(1)} %bitcast.43), channel_id=1, replica_groups=mesh['gx'=4,'gy'=8] {'gx','gy'}, dimensions={0} | all-to-all | bytes 98304 | tf_op jit(solution)/shard_map/all_to_all | solution.py:571
  58.7 0.5 shard_map.127
  59.2 9.0 %all_to_all.60 = f32[32,1,384]{2,1,0:T(1,128)S(1)} all-to-all(f32[32,1,384]{2,1,0:T(1,128)S(1)} %bitcast.45), channel_id=1, replica_groups=mesh['gx'=4,'gy'=8] {'gx','gy'}, dimensions={0} | all-to-all | bytes 98304 | tf_op jit(solution)/shard_map/all_to_all | solution.py:571
  68.2 1.6 %shard_map.128 = (f32[8,128]{1,0:T(8,128)S(1)}, f32[8,3,16,128]{3,2,1,0:T(8,128)S(1)}, f32[8,3,16,128]{3,2,1,0:T(8,128)S(1)}, f32[8,3,16,128]{3,2,1,0:T(8,128)S(...) custom-call(f32[96,128]{1,0:T(8,128)S(1)} %bitcast.36, ...), custom_call_target="tpu_custom_call" | custom-call | tf_op jit(solution)/shard_map/pallas_call | solution.py:63
  69.8 9.0 %all_to_all.61 = f32[32,1,384]{2,1,0:T(1,128)S(1)} all-to-all(f32[32,1,384]{2,1,0:T(1,128)S(1)} %bitcast.40), channel_id=1, replica_groups=mesh['gx'=4,'gy'=8] {'gx','gy'}, dimensions={0} | all-to-all | bytes 98304 | tf_op jit(solution)/shard_map/all_to_all | solution.py:571
  78.8 0.5 shard_map.129
  79.2 9.0 %all_to_all.62 = f32[32,1,384]{2,1,0:T(1,128)S(1)} all-to-all(f32[32,1,384]{2,1,0:T(1,128)S(1)} %bitcast.46), channel_id=1, replica_groups=mesh['gx'=4,'gy'=8] {'gx','gy'}, dimensions={0} | all-to-all | bytes 98304 | tf_op jit(solution)/shard_map/all_to_all | solution.py:571
  88.3 1.6 %shard_map.130 = (f32[8,128]{1,0:T(8,128)S(1)}, f32[8,3,16,128]{3,2,1,0:T(8,128)S(1)}, f32[8,3,16,128]{3,2,1,0:T(8,128)S(1)}, f32[8,3,16,128]{3,2,1,0:T(8,128)S(...) custom-call(f32[96,128]{1,0:T(8,128)S(1)} %bitcast.28, ...), custom_call_target="tpu_custom_call" | custom-call | tf_op jit(solution)/shard_map/pallas_call | solution.py:63
  89.9 9.0 %all_to_all.63 = f32[32,1,384]{2,1,0:T(1,128)S(1)} all-to-all(f32[32,1,384]{2,1,0:T(1,128)S(1)} %bitcast.38), channel_id=1, replica_groups=mesh['gx'=4,'gy'=8] {'gx','gy'}, dimensions={0} | all-to-all | bytes 98304 | tf_op jit(solution)/shard_map/all_to_all | solution.py:571
  98.9 0.5 shard_map.131
  99.3 9.0 %all_to_all.64 = f32[32,1,384]{2,1,0:T(1,128)S(1)} all-to-all(f32[32,1,384]{2,1,0:T(1,128)S(1)} %bitcast.42), channel_id=1, replica_groups=mesh['gx'=4,'gy'=8] {'gx','gy'}, dimensions={0} | all-to-all | bytes 98304 | tf_op jit(solution)/shard_map/all_to_all | solution.py:571
  108.4 0.0 copy-start.3
  108.4 0.7 shard_map.132
  109.1 8.9 %all_to_all.65 = f32[32,1,128]{2,1,0:T(1,128)S(1)} all-to-all(f32[32,1,128]{2,1,0:T(1,128)S(1)} %bitcast.47), channel_id=1, replica_groups=mesh['gx'=4,'gy'=8] {'gx','gy'}, dimensions={0} | all-to-all | bytes 32768 | tf_op jit(solution)/shard_map/all_to_all | solution.py:571
  117.9 0.0 copy-done.3
  117.9 1.0 shard_map.133
Async XLA Ops:
  0.6 27.4 %copy-start.2 = (bf16[6,8,16,128]{3,2,1,0:T(8,128)(2,1)S(1)}, bf16[6,8,16,128]{3,2,1,0:T(8,128)(2,1)}, u32[]{:S(2)}) copy-start(bf16[6,8,16,128]{3,2,1,0:T(8,128)(2,1)} %refs_15_.3) | copy-start | bytes 589828
  0.6 27.4 %copy-start.4 = (f32[8,3,16,128]{3,2,1,0:T(8,128)S(1)}, f32[8,3,16,128]{3,2,1,0:T(8,128)}, u32[]{:S(2)}) copy-start(f32[8,3,16,128]{3,2,1,0:T(8,128)} %refs_6_.3) | copy-start | bytes 589828
  3.0 25.0 %copy-start = (bf16[4,6,6,16,128]{4,3,2,1,0:T(8,128)(2,1)S(1)}, bf16[4,6,6,16,128]{4,3,2,1,0:T(8,128)(2,1)}, u32[]{:S(2)}) copy-start(bf16[4,6,6,16,128]{4,3,2,1,0:T(8,128)(2,1)} %inverse.1) | copy-start | bytes 1769476
  17.5 10.6 %copy-start.1 = (bf16[8,3,3,16,128]{4,3,2,1,0:T(8,128)(2,1)S(1)}, bf16[8,3,3,16,128]{4,3,2,1,0:T(8,128)(2,1)}, u32[]{:S(2)}) copy-start(bf16[8,3,3,16,128]{4,3,2,1,0:T(8,128)(2,1)} %refs_14_.3) | copy-start | bytes 884740
  108.4 9.6 %copy-start.3 = (f32[8,3,16,128]{3,2,1,0:T(8,128)S(1)}, f32[8,3,16,128]{3,2,1,0:T(8,128)}, u32[]{:S(2)}) copy-start(f32[8,3,16,128]{3,2,1,0:T(8,128)} %guess.1) | copy-start | bytes 589828
